TPU v7x, 256 devices: a whole 4x4x8 slice. The times are simulated.
256 devices in a mesh: wide: 16 (over x, y_hi, core), narrow: 16 (over z, y_lo).
Axes of the slice: x: 4, y: 4 (y_hi: 2, y_lo: 2; y = y_hi * 2 + y_lo), z: 8, core: 2. Of those that a mesh axis runs over, the one named last changes fastest.
Arguments:
- entity_table: float32 [262144, 512], P(('wide', 'narrow')), may hold values from -1 to 1
- row_state: float32 [262144], P(('wide', 'narrow')), may hold values from 0.001 to 0.01
- operators: float32 [4, 512, 512], P(None, 'narrow'), may hold values from -0.25 to 0.25
- op_state: float32 [4, 512, 512], P(None, 'narrow', 'wide'), may hold values from 1 to 100
- head_index: int32 [2, 262144], P(None, ('wide', 'narrow')), may hold values from 0 to 1023
- tail_index: int32 [2, 262144], P(None, ('wide', 'narrow')), may hold values from 0 to 1023
- batch_relation: int32 [2, 1024], P(None, ('wide', 'narrow')), may hold values from 0 to 3
Outputs:
- new_table: float32 [262144, 512], P(('wide', 'narrow'))
- new_state: float32 [262144], P(('wide', 'narrow'))
- new_operators: float32 [4, 512, 512], P(None, 'narrow', 'wide')
- new_op_state: float32 [4, 512, 512], P(None, 'narrow', 'wide')
Inputs may be any that keep to these rules, and one draw needn't show every extreme that they name: `head_index`: a row of the edge's head partition. `tail_index`: a row of the bucket's tail partition.
All inputs are finite; a program needn't handle non-finite values.
Results may differ from a plain program's by a relative error of at most 0.01.
Values may be sent and summed in bfloat16 or wider, within the bound.
No kernel may reach another device: no remote copies, remote signals or barrier semaphores. Data moves between devices by JAX's collectives and lax.ppermute only.
A program may use at most 64 MiB of HBM per device.

v0:
```python
import jax
import jax.numpy as jnp
from jax import lax
from jax.sharding import PartitionSpec as P

LEARN_RATE = 0.1


def swapped(block, axis, stride):
    count = lax.axis_size(axis)
    route = []
    for low in range(count):
        high = low | 1 << stride
        if high != low and high < count:
            route += [(low, high), (high, low)]
    return lax.ppermute(block, axis, route)


def one_hot_rows(index, count):
    return (index[:, None] == jnp.arange(count, dtype=jnp.int32)[None, :]).astype(jnp.float32)


def bucket_terms(heads_bf, tails_bf, operators_bf, head_rows, tail_rows, relations):
    batches = relations.shape[0]
    picked = heads_bf[head_rows]
    blocked = picked.reshape(batches, -1, picked.shape[1])
    chosen = operators_bf[relations]
    query = jnp.einsum("bej,bij->bei", blocked, chosen, preferred_element_type=jnp.float32).astype(
        jnp.bfloat16
    )
    query_rows = query.reshape(picked.shape)
    scores = jnp.einsum("ed,td->et", query_rows, tails_bf, preferred_element_type=jnp.float32)
    weights = jnp.exp(scores)
    weights = weights / jnp.sum(weights, axis=1, keepdims=True)
    score_grad = (weights - one_hot_rows(tail_rows, tails_bf.shape[0])).astype(jnp.bfloat16)
    query_grad = jnp.dot(score_grad, tails_bf, preferred_element_type=jnp.float32).astype(
        jnp.bfloat16
    )
    tail_grad = jnp.einsum(
        "et,ed->td", score_grad, query_rows, preferred_element_type=jnp.float32
    ).astype(jnp.bfloat16)
    grad_blocked = query_grad.reshape(query.shape)
    head_part = jnp.einsum(
        "bei,bij->bej", grad_blocked, chosen, preferred_element_type=jnp.float32
    ).reshape(picked.shape)
    head_grad = jnp.zeros(heads_bf.shape, jnp.float32).at[head_rows].add(head_part)
    per_batch = jnp.einsum(
        "bei,bej->bij", grad_blocked, blocked, preferred_element_type=jnp.float32
    )
    op_grad = jnp.einsum("br,bij->rij", one_hot_rows(relations, operators_bf.shape[0]), per_batch)
    return (head_grad, tail_grad, op_grad)


def body(entity_table, row_state, operators, op_state, head_index, tail_index, batch_relation):
    narrow_count = lax.axis_size("narrow")
    wide_count = lax.axis_size("wide")
    operators_bf = lax.all_gather(operators.astype(jnp.bfloat16), "narrow", axis=1, tiled=True)
    table_bf = entity_table.astype(jnp.bfloat16)
    top_bit = narrow_count.bit_length() - 2
    head_total = jnp.zeros(entity_table.shape, jnp.float32)
    op_total = jnp.zeros(operators_bf.shape, jnp.float32)
    returned = []
    for bucket, flip_bit in enumerate((0, top_bit)):
        partner_rows = swapped(table_bf, "narrow", flip_bit)
        head_grad, tail_grad, op_grad = bucket_terms(
            table_bf,
            partner_rows,
            operators_bf,
            head_index[bucket],
            tail_index[bucket],
            batch_relation[bucket],
        )
        head_total = head_total + head_grad
        op_total = op_total + op_grad
        returned.append(swapped(tail_grad, "narrow", flip_bit))
    entity_grad = head_total + returned[0].astype(jnp.float32) + returned[1].astype(jnp.float32)
    new_state = row_state + jnp.mean(entity_grad * entity_grad, axis=1)
    new_table = entity_table - LEARN_RATE * entity_grad / jnp.sqrt(new_state)[:, None]
    partial_sum = lax.psum_scatter(op_total, "wide", scatter_dimension=2, tiled=True)
    op_shard = lax.psum_scatter(partial_sum, "narrow", scatter_dimension=1, tiled=True)
    columns = operators.shape[2] // wide_count
    first_column = lax.axis_index("wide") * columns
    own_operators = lax.dynamic_slice_in_dim(operators, first_column, columns, 2)
    new_op_state = op_state + op_shard * op_shard
    new_operators = own_operators - LEARN_RATE * op_shard / jnp.sqrt(new_op_state)
    return (new_table, new_state, new_operators, new_op_state)


def solution(mesh):
    placed = (
        P(("wide", "narrow"), None),
        P(("wide", "narrow")),
        P(None, "narrow", None),
        P(None, "narrow", "wide"),
        P(None, ("wide", "narrow")),
        P(None, ("wide", "narrow")),
        P(None, ("wide", "narrow")),
    )
    return jax.shard_map(
        body,
        mesh=mesh,
        in_specs=placed,
        out_specs=(
            P(("wide", "narrow"), None),
            P(("wide", "narrow")),
            P(None, "narrow", "wide"),
            P(None, "narrow", "wide"),
        ),
        check_vma=False,
    )
```

profile of v0, /device:TPU:4, one launch (start us, length us, event | category | flops | bytes accessed | tf_op | source)
XLA Modules:
  0.0 451.9 jit_solution(9321979883127319817)
XLA Ops:
  7.2 1.6 convert_element_type.45
  8.9 1.7 convert_element_type.44
  10.7 1.7 collective-permute-start
  12.3 7.2 %collective-permute-start.1 = (bf16[1024,512]{1,0:T(8,128)(2,1)S(1)}, bf16[1024,512]{1,0:T(8,128)(2,1)}, u32[]{:S(2)}, u32[]{:S(2)}) collective-permute-start(bf16[1024,512]{1,0:T(8,128)(2,1)S(1)} %convert_element_type.44), channel_id=1, source_target_pairs={{0,8},{8,0},{1,9},{9,1},{2,10},{10,2},{3,11},{11,3},{4,12},{12,4},... | collective-permute-start | bytes 3145736 | tf_op jit(solution)/shard_map/ppermute | solution.py:16
  19.6 5.1 %gather_fusion = bf16[1024,512]{1,0:T(8,128)(2,1)} fusion(bf16[1024,512]{1,0:T(8,128)(2,1)S(1)} %convert_element_type.44, s32[1024]{0:T(1024)S(1)} %broadcast_clamp_fusion.1), kind=kCustom, calls=%fused_computation | custom fusion | bytes 2101248 | tf_op jit(solution)/shard_map/gather | solution.py:25
  24.7 5.1 %gather_fusion.2 = bf16[1024,512]{1,0:T(8,128)(2,1)} fusion(bf16[1024,512]{1,0:T(8,128)(2,1)S(1)} %convert_element_type.44, s32[1024]{0:T(1024)S(1)} %broadcast_clamp_fusion), kind=kCustom, calls=%fused_computation.2 | custom fusion | bytes 2101248 | tf_op jit(solution)/shard_map/gather | solution.py:25
  29.8 68.8 %all-gather.2.cloned.1.call-done = bf16[4,512,512]{2,1,0:T(8,128)(2,1)} async-done(((bf16[4,32,512]{2,1,0:T(8,128)(2,1)}), bf16[4,512,512]{2,1,0:T(8,128)(2,1)}) %all-gather.2.cloned.1.call-update) | async-done | bytes 2097168 | tf_op jit(solution)/shard_map/all_gather | solution.py:57
  98.6 2.3 gather_fusion.3
  100.9 2.0 convolution_convert_fusion.3
  102.9 2.9 exponential_reduce_fusion
  105.8 2.3 subtract_convert_fusion
  108.1 3.7 gather_fusion.1
  111.8 3.2 convolution_convert_fusion.2
  118.0 2.9 exponential_reduce_fusion.1
  122.0 3.3 convolution_convert_fusion.4
  126.0 1.7 fusion
  127.7 4.3 fusion.4
  132.0 7.2 %copy.24 = f32[4,512,512]{1,0,2:T(4,128)} copy(f32[4,512,512]{2,0,1:T(4,128)} %fusion.4) | data formatting | bytes 8388608 | tf_op jit(solution)/shard_map/add | solution.py:74
  139.3 4.2 convolution_convert_fusion.1
  143.6 2.2 convolution_convert_fusion
  145.8 1.6 collective-permute-start.2
  147.5 1.6 collective-permute-start.3
  152.5 3.6 fusion.21
  156.1 8.8 %scatter_custom_fusion = f32[1024,512]{1,0:T(8,128)} fusion(s32[1024]{0:T(1024)S(1)} %bitcast.79, f32[1024,512]{1,0:T(8,128)} %bitcast.69, f32[]{:T(128)} %constant.10.clone.1), kind=kCustom, calls=%fused_computation.28 | custom fusion | flops 524288 | bytes 2097664 | tf_op jit(solution)/shard_map/scatter-add | solution.py:46
  164.9 2.0 fusion.22
  166.9 8.9 %scatter_custom_fusion.1 = f32[1024,512]{1,0:T(8,128)} fusion(s32[1024]{0:T(1024)S(1)} %bitcast.77, f32[1024,512]{1,0:T(8,128)} %bitcast.68, f32[]{:T(128)} %constant.10.clone.1), kind=kCustom, calls=%fused_computation.26 | custom fusion | flops 524288 | bytes 2097664 | tf_op jit(solution)/shard_map/scatter-add | solution.py:46
  175.8 9.9 %collective-permute-done.2 = bf16[1024,512]{1,0:T(8,128)(2,1)} collective-permute-done((bf16[1024,512]{1,0:T(8,128)(2,1)}, bf16[1024,512]{1,0:T(8,128)(2,1)}, u32[]{:S(2)}, u32[]{:S(2)}) %collective-permute-start.2) | collective-permute-done | bytes 1048608 | tf_op jit(solution)/shard_map/ppermute | solution.py:16
  185.7 8.4 %collective-permute-done.3 = bf16[1024,512]{1,0:T(8,128)(2,1)} collective-permute-done((bf16[1024,512]{1,0:T(8,128)(2,1)}, bf16[1024,512]{1,0:T(8,128)(2,1)}, u32[]{:S(2)}, u32[]{:S(2)}) %collective-permute-start.3) | collective-permute-done | bytes 1048608 | tf_op jit(solution)/shard_map/ppermute | solution.py:16
  194.0 2.8 multiply_reduce_fusion
  197.5 92.8 %all-reduce.5.cloned.1.call-done = f32[4,512,512]{1,0,2:T(4,128)} async-done(((f32[4,512,512]{1,0,2:T(4,128)}), f32[4,512,512]{1,0,2:T(4,128)}) %all-reduce.5.cloned.1.call-update) | async-done | bytes 4194320
  292.6 4.8 %divide_subtract_fusion = f32[1024,512]{1,0:T(8,128)} fusion(f32[1024,512]{1,0:T(8,128)} %param.7, f32[1024]{0:T(1024)S(1)} %get-tuple-element.18, bf16[1024,512]{1,0:T(8,128)(2,1)} %collective-permute-done.3, bf16[1024,512]{1,0:T(8,128)(2,1)} %collective-permute-done.2, f32[1024,512]{1,0:T(8,128)S(1)} %copy-done.1, f32[1024,512]{1,0:T(8,128)} %scatter_custom_fusion.1), kind=kLoop, calls=%fused_computation.17 | loop fusion | flops 4194304 | bytes 10489856 | tf_op jit(solution)/shard_map/sub | solution.py:78
  297.4 145.8 %all-reduce.7.cloned.1.call-done = f32[4,512,32]{2,0,1:T(4,128)} async-done(((f32[4,512,32]{2,0,1:T(4,128)}), f32[4,512,32]{2,0,1:T(4,128)}) %all-reduce.7.cloned.1.call-update) | async-done | bytes 262160
  (65 shorter events, 12.2 us)
Async XLA Ops:
  7.2 12.4 %copy-start.12 = (s32[2,1024]{1,0:T(2,128)S(1)}, s32[2,1024]{1,0:T(2,128)}, u32[]{:S(2)}) copy-start(s32[2,1024]{1,0:T(2,128)} %param.11) | copy-start | bytes 24580
  7.2 12.4 %copy-start.14 = (s32[2,4]{1,0:T(2,128)S(1)}, s32[2,4]{1,0:T(2,128)}, u32[]{:S(2)}) copy-start(s32[2,4]{1,0:T(2,128)} %param.13) | copy-start | bytes 100
  7.2 91.4 %all-gather.2.cloned.1.call-start = ((), (), s32[]{:S(2)}) async-start(), calls=%async_computation | async-start | bytes 2228224 | tf_op jit(solution)/shard_map/all_gather | solution.py:57
  8.9 281.4 %all-reduce.5.cloned.1.call-start = ((), (), s32[]{:S(2)}) async-start(), calls=%async_computation.1 | async-start | bytes 8388608
  10.7 107.4 %collective-permute-start = (bf16[1024,512]{1,0:T(8,128)(2,1)S(1)}, bf16[1024,512]{1,0:T(8,128)(2,1)}, u32[]{:S(2)}, u32[]{:S(2)}) collective-permute-start(bf16[1024,512]{1,0:T(8,128)(2,1)S(1)} %convert_element_type.44), channel_id=1, source_target_pairs={{0,1},{1,0},{2,3},{3,2},{4,5},{5,4},{6,7},{7,6},{8,9},{9,8},{10,11... | collective-permute-start | bytes 3145736 | tf_op jit(solution)/shard_map/ppermute | solution.py:16
  12.3 90.5 %collective-permute-start.1 = (bf16[1024,512]{1,0:T(8,128)(2,1)S(1)}, bf16[1024,512]{1,0:T(8,128)(2,1)}, u32[]{:S(2)}, u32[]{:S(2)}) collective-permute-start(bf16[1024,512]{1,0:T(8,128)(2,1)S(1)} %convert_element_type.44), channel_id=1, source_target_pairs={{0,8},{8,0},{1,9},{9,1},{2,10},{10,2},{3,11},{11,3},{4,12},{12,4},... | collective-permute-start | bytes 3145736 | tf_op jit(solution)/shard_map/ppermute | solution.py:16
  24.7 5.1 %copy-start.13 = (s32[2,1024]{1,0:T(2,128)S(1)}, s32[2,1024]{1,0:T(2,128)}, u32[]{:S(2)}) copy-start(s32[2,1024]{1,0:T(2,128)} %param.12) | copy-start | bytes 24580
  102.9 2.9 copy-start.8
  111.8 3.2 copy-start.3
  115.0 1.0 copy-start.4
  115.0 2.0 copy-start
  115.0 2.2 copy-start.2
  118.0 2.9 copy-start.10
  122.0 3.3 copy-start.7
  139.3 303.9 %all-reduce.7.cloned.1.call-start = ((), (), s32[]{:S(2)}) async-start(), calls=%async_computation.2 | async-start | bytes 2097152
  139.3 4.3 copy-start.6
  139.3 4.3 copy-start.9
  143.6 5.5 %copy-start.17 = (u32[256]{0:T(256)S(1)}, u32[256]{0:T(256)}, u32[]{:S(2)}) copy-start(u32[256]{0:T(256)} %constant.29) | copy-start | bytes 3076
  143.6 6.1 %copy-start.16 = (u32[256]{0:T(256)S(1)}, u32[256]{0:T(256)}, u32[]{:S(2)}) copy-start(u32[256]{0:T(256)} %constant.33) | copy-start | bytes 3076
  145.8 39.9 %collective-permute-start.2 = (bf16[1024,512]{1,0:T(8,128)(2,1)}, bf16[1024,512]{1,0:T(8,128)(2,1)}, u32[]{:S(2)}, u32[]{:S(2)}) collective-permute-start(bf16[1024,512]{1,0:T(8,128)(2,1)} %convolution_convert_fusion.1), channel_id=1, source_target_pairs={{0,1},{1,0},{2,3},{3,2},{4,5},{5,4},{6,7},{7,6},{8,9},{9,8},{10,11... | collective-permute-start | bytes 3145736 | tf_op jit(solution)/shard_map/ppermute | solution.py:16
  147.5 46.6 %collective-permute-start.3 = (bf16[1024,512]{1,0:T(8,128)(2,1)}, bf16[1024,512]{1,0:T(8,128)(2,1)}, u32[]{:S(2)}, u32[]{:S(2)}) collective-permute-start(bf16[1024,512]{1,0:T(8,128)(2,1)} %convolution_convert_fusion), channel_id=1, source_target_pairs={{0,8},{8,0},{1,9},{9,1},{2,10},{10,2},{3,11},{11,3},{4,12},{12,4},... | collective-permute-start | bytes 3145736 | tf_op jit(solution)/shard_map/ppermute | solution.py:16
  156.1 8.8 %copy-start.5 = (bf16[1024,512]{1,0:T(8,128)(2,1)S(1)}, bf16[1024,512]{1,0:T(8,128)(2,1)}, u32[]{:S(2)}) copy-start(bf16[1024,512]{1,0:T(8,128)(2,1)} %copy-done.4) | copy-start | bytes 3145732
  166.9 27.1 %copy-start.1 = (f32[1024,512]{1,0:T(8,128)S(1)}, f32[1024,512]{1,0:T(8,128)}, u32[]{:S(2)}) copy-start(f32[1024,512]{1,0:T(8,128)} %scatter_custom_fusion) | copy-start | bytes 6291460
  175.8 21.1 %copy-start.15 = (f32[1024]{0:T(1024)S(1)}, f32[1024]{0:T(1024)}, u32[]{:S(2)}) copy-start(f32[1024]{0:T(1024)} %param.8) | copy-start | bytes 12292
  292.6 150.6 %copy-start.11 = (f32[4,32,32]{2,1,0:T(8,128)S(1)}, f32[4,32,32]{2,1,0:T(8,128)}, u32[]{:S(2)}) copy-start(f32[4,32,32]{2,1,0:T(8,128)} %param.10) | copy-start | bytes 49156
Sparse Core Ops, SparseCore 0:
  10.4 88.1 all-gather.1
  139.4 150.8 all-reduce.4
  292.9 150.2 all-reduce.6
where the time goes:
time: 453 us; the launch traced here: 452 us
  waiting for transfers between devices  326 us (72%)
  matrix products  34.6 us (8%)
  other arithmetic  33.5 us (7%)
  local copies, waits for them, and re-layouts  30.5 us (7%)
  between operations  15.4 us (3%)
  starting transfers between devices  12.2 us (3%)
    unnamed x5, waiting for transfers between devices  239 us
    all_gather x1, waiting for transfers between devices, body(): lax.all_gather(operators.astype(jnp.bfloat16), 'narrow', axis=1, tiled=True)  68.8 us
    ppermute x4, waiting for transfers between devices, swapped(): return lax.ppermute(block, axis, route)  18.3 us
    scatter-add x2, other arithmetic, bucket_terms(): jnp.zeros(heads_bf.shape, jnp.float32).at[head_rows].add(head_part)  17.6 us
    ppermute x4, starting transfers between devices, swapped(): return lax.ppermute(block, axis, route)  12.1 us
    gather x2, local copies, waits for them, and re-layouts, bucket_terms(): picked = heads_bf[head_rows]  10.2 us
  transfers between devices with their start and end apart: 7, of which 5 were waited for; matrix products, arithmetic and copies ran while one was open for 15% of the time, Pallas kernels for 0%

commit v1 on v0

v1 whole, which is shorter than its diff:
```python
import jax
import jax.numpy as jnp
from jax import lax
from jax.sharding import PartitionSpec as P

LEARN_RATE = 0.1


def swapped(block, axis, stride):
    count = lax.axis_size(axis)
    return lax.ppermute(block, axis, [(i, i ^ (1 << stride)) for i in range(count)])


def picks(index, count, dtype):
    return (index[:, None] == jnp.arange(count, dtype=jnp.int32)[None, :]).astype(dtype)


def spread(piece, axis):
    count = lax.axis_size(axis)
    return lax.all_to_all(jnp.broadcast_to(piece[None], (count, *piece.shape)), axis, 0, 0)


def whole_operators(operators):
    nrel, rows, width = operators.shape
    wide, narrow = lax.axis_size("wide"), lax.axis_size("narrow")
    pieces = operators.astype(jnp.bfloat16).reshape(wide, nrel * rows // wide, width)
    own = lax.dynamic_index_in_dim(pieces, lax.axis_index("wide"), 0, keepdims=False)
    across = spread(spread(own, "narrow"), "wide")
    split = across.reshape(nrel, wide // nrel, narrow, -1, width)
    return split.transpose(0, 2, 1, 3, 4).reshape(nrel, rows * narrow, width)


def bucket_terms(heads_bf, tails_bf, operators_bf, head_rows, tail_rows, relations):
    batches = relations.shape[0]
    chosen_rows = picks(head_rows, heads_bf.shape[0], jnp.bfloat16)
    picked = jnp.dot(chosen_rows, heads_bf, preferred_element_type=jnp.bfloat16)
    blocked = picked.reshape(batches, -1, picked.shape[1])
    chosen = operators_bf[relations]
    query = jnp.einsum("bej,bij->bei", blocked, chosen, preferred_element_type=jnp.float32).astype(
        jnp.bfloat16
    )
    query_rows = query.reshape(picked.shape)
    scores = jnp.einsum("ed,td->et", query_rows, tails_bf, preferred_element_type=jnp.float32)
    weights = jnp.exp(scores)
    weights = weights / jnp.sum(weights, axis=1, keepdims=True)
    target = picks(tail_rows, tails_bf.shape[0], jnp.float32)
    score_grad = (weights - target).astype(jnp.bfloat16)
    tail_grad = jnp.einsum(
        "et,ed->td", score_grad, query_rows, preferred_element_type=jnp.float32
    ).astype(jnp.bfloat16)
    query_grad = jnp.dot(score_grad, tails_bf, preferred_element_type=jnp.float32).astype(
        jnp.bfloat16
    )
    grad_blocked = query_grad.reshape(query.shape)
    head_part = jnp.einsum(
        "bei,bij->bej", grad_blocked, chosen, preferred_element_type=jnp.float32
    ).reshape(picked.shape)
    head_grad = jnp.einsum(
        "et,ed->td",
        chosen_rows,
        head_part.astype(jnp.bfloat16),
        preferred_element_type=jnp.float32,
    )
    per_batch = jnp.einsum(
        "bej,bei->bji", blocked, grad_blocked, preferred_element_type=jnp.float32
    )
    op_grad = jnp.einsum("br,bji->rji", picks(relations, operators_bf.shape[0], jnp.float32), per_batch)
    return (head_grad, tail_grad, op_grad)


def reduced_op_grad(op_total):
    nrel, width, _ = op_total.shape
    wide, narrow = lax.axis_size("wide"), lax.axis_size("narrow")
    sent = op_total.astype(jnp.bfloat16).reshape(nrel, wide, width // wide, width)
    got = lax.all_to_all(sent.transpose(1, 0, 2, 3), "wide", 0, 0)
    part = jnp.sum(got.astype(jnp.float32), axis=0).reshape(-1, width).T
    part = part.astype(jnp.bfloat16).reshape(narrow, width // narrow, part.shape[1])
    got = lax.all_to_all(part, "narrow", 0, 0)
    total = jnp.sum(got.astype(jnp.float32), axis=0)
    return total.reshape(width // narrow, nrel, width // wide).transpose(1, 0, 2)


def body(entity_table, row_state, operators, op_state, head_index, tail_index, batch_relation):
    narrow_count = lax.axis_size("narrow")
    wide_count = lax.axis_size("wide")
    table_bf = entity_table.astype(jnp.bfloat16)
    top_bit = narrow_count.bit_length() - 2
    flips = (0, top_bit)
    tails = [None, None]
    for bucket in (1, 0):
        tails[bucket] = swapped(table_bf, "narrow", flips[bucket])
    operators_bf = whole_operators(operators)
    head_total = jnp.zeros(entity_table.shape, jnp.float32)
    op_total = jnp.zeros(operators_bf.shape, jnp.float32)
    returned = [None, None]
    for bucket in (1, 0):
        head_grad, tail_grad, op_grad = bucket_terms(
            table_bf,
            tails[bucket],
            operators_bf,
            head_index[bucket],
            tail_index[bucket],
            batch_relation[bucket],
        )
        head_total = head_total + head_grad
        op_total = op_total + op_grad
        returned[bucket] = swapped(tail_grad, "narrow", flips[bucket])
    op_shard = reduced_op_grad(op_total)
    entity_grad = head_total + returned[0].astype(jnp.float32) + returned[1].astype(jnp.float32)
    new_state = row_state + jnp.mean(entity_grad * entity_grad, axis=1)
    new_table = entity_table - LEARN_RATE * entity_grad / jnp.sqrt(new_state)[:, None]
    columns = operators.shape[2] // wide_count
    first_column = lax.axis_index("wide") * columns
    own_operators = lax.dynamic_slice_in_dim(operators, first_column, columns, 2)
    new_op_state = op_state + op_shard * op_shard
    new_operators = own_operators - LEARN_RATE * op_shard / jnp.sqrt(new_op_state)
    return (new_table, new_state, new_operators, new_op_state)


def solution(mesh):
    placed = (
        P(("wide", "narrow"), None),
        P(("wide", "narrow")),
        P(None, "narrow", None),
        P(None, "narrow", "wide"),
        P(None, ("wide", "narrow")),
        P(None, ("wide", "narrow")),
        P(None, ("wide", "narrow")),
    )
    return jax.shard_map(
        body,
        mesh=mesh,
        in_specs=placed,
        out_specs=(
            P(("wide", "narrow"), None),
            P(("wide", "narrow")),
            P(None, "narrow", "wide"),
            P(None, "narrow", "wide"),
        ),
        check_vma=False,
    )
```

time: 453 us -> 190 us (0.42)
  waiting for transfers between devices: 326 us -> 67.9 us
  other arithmetic: 33.5 us -> 10.8 us
  starting transfers between devices: 12.2 us -> 34.7 us
  blocking collectives: 0 us -> 19 us
  between operations: 15.4 us -> 1.04 us
  local copies, waits for them, and re-layouts: 30.5 us -> 19.1 us
    unnamed x5 -> x0, waiting for transfers between devices: 239 us -> none
    all_gather x1 -> x0, waiting for transfers between devices: 68.8 us -> none  [body(): lax.all_gather(operators.astype(jnp.bfloat16), 'narrow', axis=1, tiled=True)]
    ppermute x4, waiting for transfers between devices: 18.3 us -> 47.4 us  [swapped(): lax.ppermute(block, axis, [(i, i ^ 1 << stride) for i in range(count)])]
    all_to_all x0 -> x3, starting transfers between devices: none -> 25.4 us  [the longest x1 10.8 us: reduced_op_grad(): got = lax.all_to_all(part, 'narrow', 0, 0)]
    all_to_all x0 -> x3, waiting for transfers between devices: none -> 20.5 us  [the longest x1 17.2 us: spread(): lax.all_to_all(jnp.broadcast_to(piece[None], (count, *piece.shape)), axis...]
    all_to_all x0 -> x1, blocking collectives: none -> 19 us  [spread(): lax.all_to_all(jnp.broadcast_to(piece[None], (count, *piece.shape)), axis...]
    scatter-add x2 -> x0, other arithmetic: 17.6 us -> none  [bucket_terms(): jnp.zeros(heads_bf.shape, jnp.float32).at[head_rows].add(head_part)]
    gather x2 -> x0, local copies, waits for them, and re-layouts: 10.2 us -> none  [bucket_terms(): picked = heads_bf[head_rows]]
  transfers between devices with their start and end apart: 7 -> 7, of which waited for: 5 -> 5; matrix products, arithmetic and copies ran while one was open for 15% -> 22% of each run, Pallas kernels for 0% -> 0%
where the time goes in v1:
time: 190 us; the launch traced here: 189 us
  waiting for transfers between devices  67.9 us (36%)
  matrix products  36.6 us (19%)
  starting transfers between devices  34.7 us (18%)
  local copies, waits for them, and re-layouts  19.1 us (10%)
  blocking collectives  19 us (10%)
  other arithmetic  10.8 us (6%)
    ppermute x4, waiting for transfers between devices, swapped(): lax.ppermute(block, axis, [(i, i ^ 1 << stride) for i in range(count)])  47.4 us
    all_to_all x1, blocking collectives, spread(): lax.all_to_all(jnp.broadcast_to(piece[None], (count, *piece.shape)), axis...  19 us
    all_to_all x1, waiting for transfers between devices, spread(): lax.all_to_all(jnp.broadcast_to(piece[None], (count, *piece.shape)), axis...  17.2 us
    all_to_all x1, starting transfers between devices, reduced_op_grad(): got = lax.all_to_all(part, 'narrow', 0, 0)  10.8 us
    ppermute x4, starting transfers between devices, swapped(): lax.ppermute(block, axis, [(i, i ^ 1 << stride) for i in range(count)])  9.26 us
    all_to_all x1, starting transfers between devices, reduced_op_grad(): got = lax.all_to_all(sent.transpose(1, 0, 2, 3), 'wide', 0, 0)  7.35 us
    all_to_all x1, starting transfers between devices, spread(): lax.all_to_all(jnp.broadcast_to(piece[None], (count, *piece.shape)), axis...  7.29 us
    unnamed x40, local copies, waits for them, and re-layouts  6.56 us
  transfers between devices with their start and end apart: 7, of which 5 were waited for; matrix products, arithmetic and copies ran while one was open for 22% of the time, Pallas kernels for 0%

profile of v1, /device:TPU:4, one launch (start us, length us, event | category | flops | bytes accessed | tf_op | source)
XLA Modules:
  0.0 189.1 jit_solution(17951536251332711300)
XLA Ops:
  1.6 19.0 %all_to_all.20 = bf16[16,8,512]{2,1,0:T(8,128)(2,1)S(1)} all-to-all(bf16[16,8,512]{2,1,0:T(8,128)(2,1)S(1)} %broadcast_in_dim.7), channel_id=1, replica_groups=mesh['wide'=16,'narrow'=16] {'narrow'}, dimensions={0} | all-to-all | bytes 262144 | tf_op jit(solution)/shard_map/all_to_all | solution.py:20
  20.6 1.5 broadcast_in_dim.8
  22.1 7.3 %all-to-all-start.1 = ((bf16[16,16,8,512]{3,2,1,0:T(8,128)(2,1)}), bf16[16,16,8,512]{3,2,1,0:T(8,128)(2,1)}, u32[]{:S(2)}, u32[]{:S(2)}) async-start(bf16[16,16,8,512]{3,2,1,0:T(8,128)(2,1)} %broadcast_in_dim.8), calls=%async_computation.1 | async-start | bytes 4194304 | tf_op jit(solution)/shard_map/all_to_all | solution.py:20
  29.4 1.1 convert_element_type.72
  31.4 1.8 copy.40
  33.3 2.5 %fusion.7 = bf16[1024,512]{1,0:T(8,128)(2,1)S(1)} fusion(bf16[1024,512]{1,0:T(8,128)(2,1)} %convert_element_type.72, s32[1024]{0:T(1024)S(1)} %bitcast.100), kind=kOutput, calls=%fused_computation.16 | convolution fusion | flops 1074790400 | bytes 2101248 | tf_op jit(solution)/shard_map/dot_general | solution.py:36
  35.8 3.5 %fusion.5 = bf16[1024,512]{1,0:T(8,128)(2,1)} fusion(bf16[1024,512]{1,0:T(8,128)(2,1)} %convert_element_type.72, s32[1024]{0:T(1024)S(1)} %bitcast.102), kind=kOutput, calls=%fused_computation.11 | convolution fusion | flops 1074790400 | bytes 2101248 | tf_op jit(solution)/shard_map/dot_general | solution.py:36
  39.3 17.2 %all-to-all-done.1 = bf16[16,16,8,512]{3,2,1,0:T(8,128)(2,1)} async-done(((bf16[16,16,8,512]{3,2,1,0:T(8,128)(2,1)}), bf16[16,16,8,512]{3,2,1,0:T(8,128)(2,1)}, u32[]{:S(2)}, u32[]{:S(2)}) %all-to-all-start.1) | async-done | bytes 2097184 | tf_op jit(solution)/shard_map/all_to_all | solution.py:20
  56.5 3.2 %copy.37 = bf16[4,16,4,8,512]{4,3,2,1,0:T(8,128)(2,1)} copy(bf16[4,16,4,8,512]{4,3,1,2,0:T(8,128)(2,1)} %bitcast.5) | data formatting | bytes 4194304 | tf_op jit(solution)/shard_map/transpose | solution.py:30
  59.7 2.3 %gather_fusion = bf16[4,512,512]{2,1,0:T(8,128)(2,1)S(1)} fusion(bf16[4,512,512]{2,1,0:T(8,128)(2,1)} %bitcast.79, s32[1024]{0:T(1024)S(1)} %pad_clamp_fusion.1), kind=kCustom, calls=%fused_computation | custom fusion | bytes 4194320 | tf_op jit(solution)/shard_map/gather | solution.py:38
  62.0 3.6 %gather_fusion.1 = bf16[4,512,512]{2,1,0:T(8,128)(2,1)} fusion(bf16[4,512,512]{2,1,0:T(8,128)(2,1)} %bitcast.80, s32[1024]{0:T(1024)S(1)} %pad_clamp_fusion), kind=kCustom, calls=%fused_computation.1 | custom fusion | bytes 4194320 | tf_op jit(solution)/shard_map/gather | solution.py:38
  66.3 8.7 %collective-permute-done = bf16[1024,512]{1,0:T(8,128)(2,1)} collective-permute-done((bf16[1024,512]{1,0:T(8,128)(2,1)}, bf16[1024,512]{1,0:T(8,128)(2,1)}, u32[]{:S(2)}, u32[]{:S(2)}) %collective-permute-start) | collective-permute-done | bytes 1048608 | tf_op jit(solution)/shard_map/ppermute | solution.py:11
  75.1 2.7 %exponential_reduce_fusion.1 = (f32[1024]{0:T(1024)S(1)}, f32[1024,1024]{0,1:T(8,128)S(1)}) fusion(bf16[1024,512]{1,0:T(8,128)(2,1)S(1)} %bitcast.93, bf16[1024,512]{1,0:T(8,128)(2,1)} %collective-permute-done), kind=kOutput, calls=%fused_computation.18 | convolution fusion | flops 1074789376 | bytes 6295552 | tf_op jit(solution)/shard_map/ed,td->et/dot_general | solution.py:43
  78.5 1.0 subtract_convert_fusion.1
  79.5 2.3 %convolution_convert_fusion = bf16[1024,512]{0,1:T(8,128)(2,1)} fusion(bf16[1024,1024]{0,1:T(8,128)(2,1)S(1)} %subtract_convert_fusion.1, bf16[1024,512]{1,0:T(8,128)(2,1)S(1)} %bitcast.94), kind=kOutput, calls=%fused_computation.26 | convolution fusion | flops 1074266112 | bytes 4194304 | tf_op jit(solution)/shard_map/et,ed->td/dot_general | solution.py:48
  81.9 2.5 %exponential_reduce_fusion = (f32[1024]{0:T(1024)S(1)}, f32[1024,1024]{0,1:T(8,128)S(1)}) fusion(bf16[1024,512]{1,0:T(8,128)(2,1)S(1)} %bitcast.90, bf16[1024,512]{1,0:T(8,128)(2,1)} %collective-permute-done.1), kind=kOutput, calls=%fused_computation.17 | convolution fusion | flops 1074789376 | bytes 6295552 | tf_op jit(solution)/shard_map/ed,td->et/dot_general | solution.py:43
  85.4 3.3 %convolution_convert_fusion.3 = bf16[1024,512]{1,0:T(8,128)(2,1)S(1)} fusion(bf16[1024,1024]{0,1:T(8,128)(2,1)S(1)} %subtract_convert_fusion, bf16[1024,512]{1,0:T(8,128)(2,1)} %collective-permute-done.1), kind=kOutput, calls=%fused_computation.29 | convolution fusion | flops 1074266112 | bytes 4194304 | tf_op jit(solution)/shard_map/dot_general | solution.py:51
  89.7 2.7 %convolution_convert_fusion.6 = bf16[1024,512]{1,0:T(8,128)(2,1)S(1)} fusion(bf16[1024,1024]{0,1:T(8,128)(2,1)S(1)} %subtract_convert_fusion.1, bf16[1024,512]{1,0:T(8,128)(2,1)} %collective-permute-done), kind=kOutput, calls=%fused_computation.32 | convolution fusion | flops 1074266112 | bytes 4194304 | tf_op jit(solution)/shard_map/dot_general | solution.py:51
  93.5 1.7 fusion
  95.2 3.4 %add_convert_fusion = bf16[4,512,512]{2,0,1:T(4,128)(2,1)} fusion(f32[4,512,512]{2,0,1:T(4,128)S(1)} %fusion, bf16[4,512,512]{2,1,0:T(8,128)(2,1)S(1)} %fusion.25, s32[4]{0:T(128)S(1)} %get-tuple-element.30), kind=kOutput, calls=%fused_computation.6 | convolution fusion | flops 10485776 | bytes 8388624 | tf_op jit(solution)/shard_map/br,bji->rji/dot_general | solution.py:67
  98.6 7.3 %all-to-all-start.2 = ((bf16[16,4,32,512]{3,1,2,0:T(4,128)(2,1)}), bf16[16,4,32,512]{3,1,2,0:T(4,128)(2,1)}, u32[]{:S(2)}, u32[]{:S(2)}) async-start(bf16[16,4,32,512]{3,1,2,0:T(4,128)(2,1)} %bitcast.81), calls=%async_computation.2 | async-start | bytes 4194304 | tf_op jit(solution)/shard_map/all_to_all | solution.py:75
  106.0 3.0 %convolution_convert_fusion.1 = bf16[1024,512]{0,1:T(8,128)(2,1)S(1)} fusion(bf16[1024,1024]{0,1:T(8,128)(2,1)} %copy-done.9, bf16[1024,512]{1,0:T(8,128)(2,1)S(1)} %bitcast.91), kind=kOutput, calls=%fused_computation.27 | convolution fusion | flops 1074266112 | bytes 4194304 | tf_op jit(solution)/shard_map/et,ed->td/dot_general | solution.py:48
  109.6 7.9 %collective-permute-start.2 = (bf16[1024,512]{0,1:T(8,128)(2,1)S(1)}, bf16[1024,512]{0,1:T(8,128)(2,1)S(1)}, u32[]{:S(2)}, u32[]{:S(2)}) collective-permute-start(bf16[1024,512]{0,1:T(8,128)(2,1)S(1)} %convolution_convert_fusion.1), channel_id=1, source_target_pairs={{0,1},{1,0},{2,3},{3,2},{4,5},{5,4},{6,7},{7,6},{8,9},{9,8},{10,11... | collective-permute-start | bytes 3145736 | tf_op jit(solution)/shard_map/ppermute | solution.py:11
  119.1 1.5 fusion.4
  121.3 17.3 %collective-permute-done.3 = bf16[1024,512]{0,1:T(8,128)(2,1)S(1)} collective-permute-done((bf16[1024,512]{0,1:T(8,128)(2,1)S(1)}, bf16[1024,512]{0,1:T(8,128)(2,1)S(1)}, u32[]{:S(2)}, u32[]{:S(2)}) %collective-permute-start.3) | collective-permute-done | bytes 1048608 | tf_op jit(solution)/shard_map/ppermute | solution.py:11
  138.6 21.4 %collective-permute-done.2 = bf16[1024,512]{0,1:T(8,128)(2,1)S(1)} collective-permute-done((bf16[1024,512]{0,1:T(8,128)(2,1)S(1)}, bf16[1024,512]{0,1:T(8,128)(2,1)S(1)}, u32[]{:S(2)}, u32[]{:S(2)}) %collective-permute-start.2) | collective-permute-done | bytes 1048608 | tf_op jit(solution)/shard_map/ppermute | solution.py:11
  160.0 3.1 %multiply_reduce_fusion = (f32[1024]{0:T(1024)S(1)}, f32[1024,512]{0,1:T(8,128)}) fusion(bf16[1024,512]{0,1:T(8,128)(2,1)S(1)} %collective-permute-done.3, bf16[1024,512]{0,1:T(8,128)(2,1)S(1)} %collective-permute-done.2, f32[1024,512]{0,1:T(8,128)S(1)} %fusion.4, bf16[1024,512]{1,0:T(8,128)(2,1)S(1)} %bitcast.92, s32[1024]{0:T(1024)S(1)} %bitcast.101), kind=kOutput, calls=%fused_computation.20 | convolution fusion | flops 1078459392 | bytes 7348224 | tf_op jit(solution)/shard_map/et,ed->td/dot_general | solution.py:58
  163.7 2.5 %reduce_sum.51 = bf16[4,32,512]{2,0,1:T(4,128)(2,1)S(1)} reduce(bf16[16,4,32,512]{3,1,2,0:T(4,128)(2,1)} %all-to-all-done.2, bf16[]{:T(256)} %constant.28.clone.1), dimensions={0}, to_apply=%region_3.4 | reduce | flops 983040 | bytes 2228226 | tf_op jit(solution)/shard_map/reduce_sum | solution.py:76
  167.0 10.8 %all-to-all-start.3 = ((bf16[16,32,128]{2,1,0:T(8,128)(2,1)}), bf16[16,32,128]{2,1,0:T(8,128)(2,1)S(1)}, u32[]{:S(2)}, u32[]{:S(2)}) async-start(bf16[16,32,128]{2,1,0:T(8,128)(2,1)} %bitcast.29), calls=%async_computation.3 | async-start | bytes 262144 | tf_op jit(solution)/shard_map/all_to_all | solution.py:78
  177.8 3.4 %divide_subtract_fusion = f32[1024,512]{0,1:T(8,128)} fusion(f32[1024,512]{0,1:T(8,128)S(1)} %copy-done.3, f32[1024,512]{0,1:T(8,128)} %get-tuple-element.39, f32[1024]{0:T(1024)S(1)} %get-tuple-element.22), kind=kLoop, calls=%fused_computation.19 | loop fusion | flops 1572864 | bytes 6295552 | tf_op jit(solution)/shard_map/sub | solution.py:111
  181.2 2.9 %copy.49 = f32[1024,512]{1,0:T(8,128)} copy(f32[1024,512]{0,1:T(8,128)} %divide_subtract_fusion) | data formatting | bytes 4194304
  184.1 3.3 %all-to-all-done.3 = bf16[16,32,128]{2,1,0:T(8,128)(2,1)S(1)} async-done(((bf16[16,32,128]{2,1,0:T(8,128)(2,1)}), bf16[16,32,128]{2,1,0:T(8,128)(2,1)S(1)}, u32[]{:S(2)}, u32[]{:S(2)}) %all-to-all-start.3) | async-done | bytes 131104 | tf_op jit(solution)/shard_map/all_to_all | solution.py:78
  (68 shorter events, 12.3 us)
Async XLA Ops:
  22.1 7.3 %copy-start.2 = (f32[1024,512]{1,0:T(8,128)S(1)}, f32[1024,512]{1,0:T(8,128)}, u32[]{:S(2)}) copy-start(f32[1024,512]{1,0:T(8,128)} %param.7) | copy-start | bytes 6291460
  22.1 34.3 %all-to-all-start.1 = ((bf16[16,16,8,512]{3,2,1,0:T(8,128)(2,1)}), bf16[16,16,8,512]{3,2,1,0:T(8,128)(2,1)}, u32[]{:S(2)}, u32[]{:S(2)}) async-start(bf16[16,16,8,512]{3,2,1,0:T(8,128)(2,1)} %broadcast_in_dim.8), calls=%async_computation.1 | async-start | bytes 4194304 | tf_op jit(solution)/shard_map/all_to_all | solution.py:20
  30.6 2.6 %copy-start.15 = (s32[2,4]{1,0:T(2,128)S(1)}, s32[2,4]{1,0:T(2,128)}, u32[]{:S(2)}) copy-start(s32[2,4]{1,0:T(2,128)} %param.13) | copy-start | bytes 100
  30.6 2.7 %copy-start.13 = (s32[2,1024]{1,0:T(2,128)S(1)}, s32[2,1024]{1,0:T(2,128)}, u32[]{:S(2)}) copy-start(s32[2,1024]{1,0:T(2,128)} %param.11) | copy-start | bytes 24580
  30.6 2.7 %copy-start.14 = (s32[2,1024]{1,0:T(2,128)S(1)}, s32[2,1024]{1,0:T(2,128)}, u32[]{:S(2)}) copy-start(s32[2,1024]{1,0:T(2,128)} %param.12) | copy-start | bytes 24580
  30.6 44.5 %collective-permute-start = (bf16[1024,512]{1,0:T(8,128)(2,1)}, bf16[1024,512]{1,0:T(8,128)(2,1)}, u32[]{:S(2)}, u32[]{:S(2)}) collective-permute-start(bf16[1024,512]{1,0:T(8,128)(2,1)} %convert_element_type.72), channel_id=1, source_target_pairs={{0,8},{1,9},{2,10},{3,11},{4,12},{5,13},{6,14},{7,15},{8,0},{9,1},... | collective-permute-start | bytes 3145736 | tf_op jit(solution)/shard_map/ppermute | solution.py:11
  31.4 50.5 %collective-permute-start.1 = (bf16[1024,512]{1,0:T(8,128)(2,1)}, bf16[1024,512]{1,0:T(8,128)(2,1)}, u32[]{:S(2)}, u32[]{:S(2)}) collective-permute-start(bf16[1024,512]{1,0:T(8,128)(2,1)} %convert_element_type.72), channel_id=1, source_target_pairs={{0,1},{1,0},{2,3},{3,2},{4,5},{5,4},{6,7},{7,6},{8,9},{9,8},{10,11... | collective-permute-start | bytes 3145736 | tf_op jit(solution)/shard_map/ppermute | solution.py:11
  75.1 2.7 %copy-start = (bf16[4,512,512]{2,1,0:T(8,128)(2,1)S(1)}, bf16[4,512,512]{2,1,0:T(8,128)(2,1)}, u32[]{:S(2)}) copy-start(bf16[4,512,512]{2,1,0:T(8,128)(2,1)} %gather_fusion.1) | copy-start | bytes 6291460
  75.1 2.7 %copy-start.4 = (bf16[1024,512]{1,0:T(8,128)(2,1)S(1)}, bf16[1024,512]{1,0:T(8,128)(2,1)}, u32[]{:S(2)}) copy-start(bf16[1024,512]{1,0:T(8,128)(2,1)} %fusion.5) | copy-start | bytes 3145732
  78.5 3.4 %copy-start.10 = (bf16[4,256,512]{2,1,0:T(8,128)(2,1)}, bf16[4,256,512]{2,1,0:T(8,128)(2,1)S(1)}, u32[]{:S(2)}) copy-start(bf16[4,256,512]{2,1,0:T(8,128)(2,1)S(1)} %convolution_convert_fusion.4) | copy-start | bytes 3145732
  85.4 3.3 %copy-start.9 = (bf16[1024,1024]{0,1:T(8,128)(2,1)}, bf16[1024,1024]{0,1:T(8,128)(2,1)S(1)}, u32[]{:S(2)}) copy-start(bf16[1024,1024]{0,1:T(8,128)(2,1)S(1)} %subtract_convert_fusion) | copy-start | bytes 6291460
  88.7 1.1 copy-start.7
  92.5 1.0 copy-start.5
  98.6 7.4 %copy-start.11 = (bf16[4,256,512]{2,1,0:T(8,128)(2,1)S(1)}, bf16[4,256,512]{2,1,0:T(8,128)(2,1)}, u32[]{:S(2)}) copy-start(bf16[4,256,512]{2,1,0:T(8,128)(2,1)} %copy-done.10) | copy-start | bytes 3145732
  98.6 65.1 %all-to-all-start.2 = ((bf16[16,4,32,512]{3,1,2,0:T(4,128)(2,1)}), bf16[16,4,32,512]{3,1,2,0:T(4,128)(2,1)}, u32[]{:S(2)}, u32[]{:S(2)}) async-start(bf16[16,4,32,512]{3,1,2,0:T(4,128)(2,1)} %bitcast.81), calls=%async_computation.2 | async-start | bytes 4194304 | tf_op jit(solution)/shard_map/all_to_all | solution.py:75
  105.9 3.1 %copy-start.17 = (bf16[1024,512]{0,1:T(8,128)(2,1)S(1)}, bf16[1024,512]{0,1:T(8,128)(2,1)}, u32[]{:S(2)}) copy-start(bf16[1024,512]{0,1:T(8,128)(2,1)} %convolution_convert_fusion) | copy-start | bytes 3145732
  105.9 12.4 %copy-start.1 = (bf16[4,512,512]{2,1,0:T(8,128)(2,1)S(1)}, bf16[4,512,512]{2,1,0:T(8,128)(2,1)}, u32[]{:S(2)}) copy-start(bf16[4,512,512]{2,1,0:T(8,128)(2,1)} %gather_fusion.1) | copy-start | bytes 6291460
  106.0 12.4 %copy-start.8 = (bf16[1024,512]{1,0:T(8,128)(2,1)S(1)}, bf16[1024,512]{1,0:T(8,128)(2,1)}, u32[]{:S(2)}) copy-start(bf16[1024,512]{1,0:T(8,128)(2,1)} %copy-done.7) | copy-start | bytes 3145732
  109.0 29.6 %collective-permute-start.3 = (bf16[1024,512]{0,1:T(8,128)(2,1)S(1)}, bf16[1024,512]{0,1:T(8,128)(2,1)S(1)}, u32[]{:S(2)}, u32[]{:S(2)}) collective-permute-start(bf16[1024,512]{0,1:T(8,128)(2,1)S(1)} %copy-done.17), channel_id=1, source_target_pairs={{0,8},{1,9},{2,10},{3,11},{4,12},{5,13},{6,14},{7,15},{8,0},{9,1},... | collective-permute-start | bytes 3145736 | tf_op jit(solution)/shard_map/ppermute | solution.py:11
  109.6 50.4 %collective-permute-start.2 = (bf16[1024,512]{0,1:T(8,128)(2,1)S(1)}, bf16[1024,512]{0,1:T(8,128)(2,1)S(1)}, u32[]{:S(2)}, u32[]{:S(2)}) collective-permute-start(bf16[1024,512]{0,1:T(8,128)(2,1)S(1)} %convolution_convert_fusion.1), channel_id=1, source_target_pairs={{0,1},{1,0},{2,3},{3,2},{4,5},{5,4},{6,7},{7,6},{8,9},{9,8},{10,11... | collective-permute-start | bytes 3145736 | tf_op jit(solution)/shard_map/ppermute | solution.py:11
  119.1 1.5 copy-start.6
  160.0 3.1 %copy-start.16 = (f32[1024]{0:T(1024)S(1)}, f32[1024]{0:T(1024)}, u32[]{:S(2)}) copy-start(f32[1024]{0:T(1024)} %param.8) | copy-start | bytes 12292
  163.1 14.7 %copy-start.3 = (f32[1024,512]{0,1:T(8,128)S(1)}, f32[1024,512]{0,1:T(8,128)}, u32[]{:S(2)}) copy-start(f32[1024,512]{0,1:T(8,128)} %copy.40) | copy-start | bytes 6291460
  167.0 20.4 %all-to-all-start.3 = ((bf16[16,32,128]{2,1,0:T(8,128)(2,1)}), bf16[16,32,128]{2,1,0:T(8,128)(2,1)S(1)}, u32[]{:S(2)}, u32[]{:S(2)}) async-start(bf16[16,32,128]{2,1,0:T(8,128)(2,1)} %bitcast.29), calls=%async_computation.3 | async-start | bytes 262144 | tf_op jit(solution)/shard_map/all_to_all | solution.py:78
  181.2 6.5 %copy-start.12 = (f32[4,32,32]{2,1,0:T(8,128)S(1)}, f32[4,32,32]{2,1,0:T(8,128)}, u32[]{:S(2)}) copy-start(f32[4,32,32]{2,1,0:T(8,128)} %param.10) | copy-start | bytes 49156

commit v2 on v0

v2 whole, which is shorter than its diff:
```python
import jax
import jax.numpy as jnp
from jax import lax
from jax.experimental import pallas as pl
from jax.experimental.pallas import tpu as pltpu
from jax.sharding import PartitionSpec as P


LEARN_RATE = 0.1
BF = jnp.bfloat16
F32 = jnp.float32
NN = (((1,), (0,)), ((), ()))
NT = (((1,), (1,)), ((), ()))
TN = (((0,), (0,)), ((), ()))


def dot(a, b, dims):
    return lax.dot_general(a, b, dims, preferred_element_type=F32)


def swapped(block, axis, stride):
    count = lax.axis_size(axis)
    return lax.ppermute(block, axis, [(i, i ^ (1 << stride)) for i in range(count)])


def same_core():
    return [list(range(core, lax.axis_size("wide"), 2)) for core in range(2)]


def spread(piece, count, axis, groups=None):
    sent = jnp.broadcast_to(piece[None], (count, *piece.shape))
    return lax.all_to_all(sent, axis, 0, 0, axis_index_groups=groups)


def whole_operators(operators):
    nrel, rows, width = operators.shape
    chips, narrow = lax.axis_size("wide") // 2, lax.axis_size("narrow")
    place = lax.axis_index("wide")
    chip, core = place // 2, place % 2
    high, half = nrel * rows // chips, width // 2
    pieces = operators.astype(BF).reshape(chips, high, width)
    own = lax.dynamic_index_in_dim(pieces, chip, 0, keepdims=False)
    own = lax.dynamic_slice_in_dim(own, core * half, half, 1)
    across = spread(own, narrow, "narrow")
    across = spread(across, chips, "wide", same_core())
    other = swapped(across, "wide", 0)
    first = jnp.where(core == 0, across, other)
    second = jnp.where(core == 0, other, across)
    full = jnp.concatenate([first, second], axis=-1)
    full = full.reshape(nrel, chips // nrel, narrow, high, width)
    return full.transpose(0, 2, 1, 3, 4).reshape(nrel, rows * narrow, width)


def forward_kernel(relations, heads, tails, operators, head_at, tail_at, rows, query_grad, tail_grad, total):
    batches = relations.shape[0]
    edges = rows.shape[0] // batches
    count = tails.shape[0]

    def one(batch, carry):
        at = pl.ds(pl.multiple_of(batch * edges, edges), edges)
        lane = lax.broadcasted_iota(jnp.int32, (edges, count), 1)
        picks = (head_at[at, :] == lane).astype(F32).astype(BF)
        row = dot(picks, heads[...], NN).astype(BF)
        rows[at, :] = row
        query = dot(row, operators[relations[batch]], NT).astype(BF)
        weights = jnp.exp(dot(query, tails[...], NT))
        weights = weights * (1.0 / jnp.sum(weights, axis=1, keepdims=True))
        grad = (weights - (tail_at[at, :] == lane).astype(F32)).astype(BF)
        part = dot(grad, query, TN)

        @pl.when(batch == 0)
        def _():
            total[...] = part

        @pl.when(batch > 0)
        def _():
            total[...] += part

        query_grad[at, :] = dot(grad, tails[...], NN).astype(BF)
        return carry

    lax.fori_loop(0, batches, one, 0)
    tail_grad[...] = total[...].astype(BF)


def vmem():
    return pl.BlockSpec(memory_space=pltpu.VMEM)


def smem():
    return pl.BlockSpec(memory_space=pltpu.SMEM)


def forward(heads, tails, operators, head_at, tail_at, relations):
    edges, (count, width) = head_at.shape[0], heads.shape
    return pl.pallas_call(
        forward_kernel,
        out_shape=(
            jax.ShapeDtypeStruct((edges, width), BF),
            jax.ShapeDtypeStruct((edges, width), BF),
            jax.ShapeDtypeStruct((count, width), BF),
        ),
        in_specs=[smem()] + [vmem()] * 5,
        out_specs=(vmem(), vmem(), vmem()),
        scratch_shapes=[pltpu.VMEM((count, width), F32)],
        cost_estimate=pl.CostEstimate(
            flops=9 * edges * count * width, bytes_accessed=16 * count * width, transcendentals=edges * count
        ),
        name="forward",
    )(relations, heads, tails, operators, head_at, tail_at)


def operator_kernel(relations, core, rows0, grad0, rows1, grad1, kept, sent, total):
    batches = relations.shape[1]
    edges = rows0.shape[0] // batches
    width = rows0.shape[1]
    nrel, chips, _, columns, _ = total.shape
    total[...] = jnp.zeros_like(total)
    for bucket, (rows, grad) in enumerate(((rows0, grad0), (rows1, grad1))):

        def one(batch, carry, bucket=bucket, rows=rows, grad=grad):
            at = pl.ds(pl.multiple_of(batch * edges, edges), edges)
            part = dot(rows[at, :], grad[at, :], TN)
            total[relations[bucket, batch]] += part.reshape(chips, 2, columns, width)
            return carry

        lax.fori_loop(0, batches, one, 0)
    for r in range(nrel):
        kept[:, r] = total[r, :, core[0]]
        sent[:, r] = total[r, :, 1 - core[0]].astype(BF)


def operator_grad(relations, core, rows, grads, nrel, wide):
    edges, width = rows[0].shape
    shape = (wide // 2, nrel, width // wide, width)
    return pl.pallas_call(
        operator_kernel,
        out_shape=(jax.ShapeDtypeStruct(shape, F32), jax.ShapeDtypeStruct(shape, BF)),
        in_specs=[smem(), smem()] + [vmem()] * 4,
        out_specs=(vmem(), vmem()),
        scratch_shapes=[pltpu.VMEM((nrel, wide // 2, 2, width // wide, width), F32)],
        cost_estimate=pl.CostEstimate(
            flops=4 * edges * width * width, bytes_accessed=20 * edges * width, transcendentals=0
        ),
        name="operator_grad",
    )(relations, core, rows[0], grads[0], rows[1], grads[1])


def head_kernel(relations, head_at, grad0, grad1, operators, total):
    batches = relations.shape[1]
    edges = grad0.shape[0] // batches
    count = total.shape[0]
    for bucket, grad in enumerate((grad0, grad1)):
        for batch in range(batches):
            at = slice(batch * edges, (batch + 1) * edges)
            part = dot(grad[at, :], operators[relations[bucket, batch]], NN).astype(BF)
            row = lax.broadcasted_iota(jnp.int32, (count, edges), 0)
            picks = (head_at[bucket : bucket + 1, at] == row).astype(F32).astype(BF)
            added = dot(picks, part, NN)
            if bucket == 0 and batch == 0:
                total[...] = added
            else:
                total[...] += added


def head_grad(relations, head_at, grads, operators):
    edges, width = grads[0].shape
    return pl.pallas_call(
        head_kernel,
        out_shape=jax.ShapeDtypeStruct((edges, width), F32),
        in_specs=[smem()] + [vmem()] * 4,
        out_specs=vmem(),
        cost_estimate=pl.CostEstimate(
            flops=6 * edges * edges * width, bytes_accessed=12 * edges * width, transcendentals=0
        ),
        name="head_grad",
    )(relations, head_at, grads[0], grads[1], operators)


def summed_over_devices(kept, sent):
    _, nrel, columns, width = kept.shape
    narrow = lax.axis_size("narrow")
    pair = (kept + swapped(sent, "wide", 0).astype(F32)).astype(BF)
    got = lax.all_to_all(pair, "wide", 0, 0, axis_index_groups=same_core())
    part = jnp.sum(got.astype(F32), axis=0).reshape(nrel * columns, width).T
    got = lax.all_to_all(part.reshape(narrow, width // narrow, nrel * columns), "narrow", 0, 0)
    total = jnp.sum(got, axis=0)
    return total.reshape(width // narrow, nrel, columns).transpose(1, 0, 2)


def step(entity_table, row_state, operators, op_state, head_index, tail_index, batch_relation):
    narrow_count = lax.axis_size("narrow")
    wide_count = lax.axis_size("wide")
    flips = (0, narrow_count.bit_length() - 2)
    table_bf = entity_table.astype(BF)
    tails = [None, None]
    for bucket in (1, 0):
        tails[bucket] = swapped(table_bf, "narrow", flips[bucket])
    operators_bf = whole_operators(operators)
    rows, query_grads, returned = [None, None], [None, None], [None, None]
    for bucket in (0, 1):
        rows[bucket], query_grads[bucket], tail_grad = forward(
            table_bf,
            tails[bucket],
            operators_bf,
            head_index[bucket][:, None],
            tail_index[bucket][:, None],
            batch_relation[bucket],
        )
        returned[bucket] = swapped(tail_grad, "narrow", flips[bucket])
    core = (lax.axis_index("wide") % 2).astype(jnp.int32).reshape(1)
    kept, sent = operator_grad(batch_relation, core, rows, query_grads, operators.shape[0], wide_count)
    op_shard = summed_over_devices(kept, sent)
    head_total = head_grad(batch_relation, head_index, query_grads, operators_bf)
    entity_grad = head_total + returned[0].astype(F32) + returned[1].astype(F32)
    new_state = row_state + jnp.mean(entity_grad * entity_grad, axis=1)
    new_table = entity_table - LEARN_RATE * entity_grad / jnp.sqrt(new_state)[:, None]
    columns = operators.shape[2] // wide_count
    first_column = lax.axis_index("wide") * columns
    own_operators = lax.dynamic_slice_in_dim(operators, first_column, columns, 2)
    new_op_state = op_state + op_shard * op_shard
    new_operators = own_operators - LEARN_RATE * op_shard / jnp.sqrt(new_op_state)
    return (new_table, new_state, new_operators, new_op_state)


def solution(mesh):
    placed = (
        P(("wide", "narrow"), None),
        P(("wide", "narrow")),
        P(None, "narrow", None),
        P(None, "narrow", "wide"),
        P(None, ("wide", "narrow")),
        P(None, ("wide", "narrow")),
        P(None, ("wide", "narrow")),
    )
    return jax.shard_map(
        step,
        mesh=mesh,
        in_specs=placed,
        out_specs=(
            P(("wide", "narrow"), None),
            P(("wide", "narrow")),
            P(None, "narrow", "wide"),
            P(None, "narrow", "wide"),
        ),
        check_vma=False,
    )
```

time: 453 us -> 190 us (0.42)
  waiting for transfers between devices: 326 us -> 43.7 us
  Pallas kernels: 0 us -> 40.7 us
  blocking collectives: 0 us -> 39.4 us
  matrix products: 34.6 us -> 0 us
  starting transfers between devices: 12.2 us -> 38.4 us
  other arithmetic: 33.5 us -> 13.8 us
  local copies, waits for them, and re-layouts: 30.5 us -> 12.6 us
  between operations: 15.4 us -> 0.85 us
    unnamed x5 -> x0, waiting for transfers between devices: 239 us -> none
    all_gather x1 -> x0, waiting for transfers between devices: 68.8 us -> none  [body(): lax.all_gather(operators.astype(jnp.bfloat16), 'narrow', axis=1, tiled=True)]
    pallas_call x0 -> x4, Pallas kernels: none -> 40.7 us  [the longest x2 25.6 us: forward(): pl.pallas_call(forward_kernel, out_shape=(jax.ShapeDtypeStruct((edges, wi...]
    all_to_all x0 -> x2, blocking collectives: none -> 39.4 us  [spread(): return lax.all_to_all(sent, axis, 0, 0, axis_index_groups=groups)]
    all_to_all x0 -> x2, starting transfers between devices: none -> 34.9 us  [the longest x1 29 us: summed_over_devices(): lax.all_to_all(part.reshape(narrow, width // narrow, nrel * columns), 'na...]
    dot_general x14 -> x0, matrix products: 34.6 us -> none  [the longest x2 6.49 us: bucket_terms(): jnp.dot(score_grad, tails_bf, preferred_element_type=jnp.float32)]
    scatter-add x2 -> x0, other arithmetic: 17.6 us -> none  [bucket_terms(): jnp.zeros(heads_bf.shape, jnp.float32).at[head_rows].add(head_part)]
    ppermute x4 -> x6, waiting for transfers between devices: 18.3 us -> 35.6 us  [swapped(): lax.ppermute(block, axis, [(i, i ^ 1 << stride) for i in range(count)])]
  transfers between devices with their start and end apart: 7 -> 8, of which waited for: 5 -> 5; matrix products, arithmetic and copies ran while one was open for 15% -> 10% of each run, Pallas kernels for 0% -> 11%
where the time goes in v2:
time: 190 us; the launch traced here: 189 us
  waiting for transfers between devices  43.7 us (23%)
  Pallas kernels  40.7 us (21%)
  blocking collectives  39.4 us (21%)
  starting transfers between devices  38.4 us (20%)
  other arithmetic  13.8 us (7%)
  local copies, waits for them, and re-layouts  12.6 us (7%)
    all_to_all x2, blocking collectives, spread(): return lax.all_to_all(sent, axis, 0, 0, axis_index_groups=groups)  39.4 us
    ppermute x6, waiting for transfers between devices, swapped(): lax.ppermute(block, axis, [(i, i ^ 1 << stride) for i in range(count)])  35.6 us
    all_to_all x1, starting transfers between devices, summed_over_devices(): lax.all_to_all(part.reshape(narrow, width // narrow, nrel * columns), 'na...  29 us
    pallas_call x2, Pallas kernels, forward(): pl.pallas_call(forward_kernel, out_shape=(jax.ShapeDtypeStruct((edges, wi...  25.6 us
    pallas_call x1, Pallas kernels, head_grad(): pl.pallas_call(head_kernel, out_shape=jax.ShapeDtypeStruct((edges, width)...  8.08 us
    all_to_all x1, waiting for transfers between devices, summed_over_devices(): lax.all_to_all(part.reshape(narrow, width // narrow, nrel * columns), 'na...  8.07 us
    pallas_call x1, Pallas kernels, operator_grad(): pl.pallas_call(operator_kernel, out_shape=(jax.ShapeDtypeStruct(shape, F3...  7.01 us
    all_to_all x1, starting transfers between devices, summed_over_devices(): got = lax.all_to_all(pair, 'wide', 0, 0, axis_index_groups=same_core())  5.85 us
  transfers between devices with their start and end apart: 8, of which 5 were waited for; matrix products, arithmetic and copies ran while one was open for 10% of the time, Pallas kernels for 11%

profile of v2, /device:TPU:4, one launch (start us, length us, event | category | flops | bytes accessed | tf_op | source)
XLA Modules:
  0.0 189.4 jit_solution(13177895616482986358)
XLA Ops:
  0.7 1.1 convert_element_type.22
  1.9 19.0 %all_to_all.20 = bf16[16,16,256]{2,1,0:T(8,128)(2,1)S(1)} all-to-all(bf16[16,16,256]{2,1,0:T(8,128)(2,1)S(1)} %broadcast_in_dim.7), channel_id=1, replica_groups=mesh['wide'=16,'narrow'=16] {'narrow'}, dimensions={0} | all-to-all | bytes 262144 | tf_op jit(solution)/shard_map/all_to_all | solution.py:32
  21.0 20.4 %all_to_all.21 = bf16[8,16,16,256]{3,2,1,0:T(8,128)(2,1)S(1)} all-to-all(bf16[8,16,16,256]{3,2,1,0:T(8,128)(2,1)S(1)} %broadcast_in_dim.8), channel_id=1, replica_groups={{0,32,64,96,128,160,192,224},{16,48,80,112,144,176,208,240},{1,33,65,97..., dimensions={0} | all-to-all | bytes 2097152 | tf_op jit(solution)/shard_map/all_to_all | solution.py:32
  41.4 1.1 convert_element_type.21.heads
  42.6 1.0 collective-permute-start.2
  44.1 1.0 copy.21.head_at
  45.2 1.0 copy.22.tail_at
  46.2 1.1 copy.23.head_at
  47.3 1.1 copy.24.tail_at
  48.3 1.4 broadcast_select_fusion.1
  50.0 1.5 copy.20
  51.5 17.0 %collective-permute-done.tails = bf16[1024,512]{1,0:T(8,128)(2,1)} collective-permute-done((bf16[1024,512]{1,0:T(8,128)(2,1)}, bf16[1024,512]{1,0:T(8,128)(2,1)}, u32[]{:S(2)}, u32[]{:S(2)}) %collective-permute-start) | collective-permute-done | bytes 1048608 | tf_op jit(solution)/shard_map/ppermute | solution.py:23
  68.4 12.8 %forward.2 = (bf16[1024,512]{1,0:T(8,128)(2,1)}, bf16[1024,512]{1,0:T(8,128)(2,1)}, bf16[1024,512]{1,0:T(8,128)(2,1)}) custom-call(s32[4]{0:T(128)} %get-tuple-element.40.relations, bf16[1024,512]{1,0:T(8,128)(2,1)} %convert_element_type.21.heads, bf16[1024,512]{1,0:T(8,128)(2,1)} %collective-permute-done.tails, bf16[4,512,512]{2,1,0:T(8,128)(2,1)} %bitcast.32, ...), custom_call_target="tpu_custom_call" | custom-call | flops 4831838208 | bytes 8388608 | tf_op jit(solution)/shard_map/forward/pallas_call | solution.py:96
  81.2 4.3 %collective-permute-done.2.tails = bf16[1024,512]{1,0:T(8,128)(2,1)S(1)} collective-permute-done((bf16[1024,512]{1,0:T(8,128)(2,1)}, bf16[1024,512]{1,0:T(8,128)(2,1)S(1)}, u32[]{:S(2)}, u32[]{:S(2)}) %collective-permute-start.2) | collective-permute-done | bytes 1048608 | tf_op jit(solution)/shard_map/ppermute | solution.py:23
  85.5 1.0 copy-done.9
  86.5 12.8 %forward.3 = (bf16[1024,512]{1,0:T(8,128)(2,1)}, bf16[1024,512]{1,0:T(8,128)(2,1)}, bf16[1024,512]{1,0:T(8,128)(2,1)}) custom-call(s32[4]{0:T(128)} %get-tuple-element.41.relations, bf16[1024,512]{1,0:T(8,128)(2,1)} %convert_element_type.21.heads, bf16[1024,512]{1,0:T(8,128)(2,1)} %copy-done.9, bf16[4,512,512]{2,1,0:T(8,128)(2,1)} %bitcast.33, ...), custom_call_target="tpu_custom_call" | custom-call | flops 4831838208 | bytes 8388608 | tf_op jit(solution)/shard_map/forward/pallas_call | solution.py:96
  99.3 7.0 %operator_grad.1 = (f32[8,4,32,512]{3,2,1,0:T(8,128)}, bf16[8,4,32,512]{3,2,1,0:T(8,128)(2,1)}) custom-call(s32[2,4]{1,0:T(2,128)} %relations.3, s32[1]{0:T(128)} %bitcast.11.core, bf16[1024,512]{1,0:T(8,128)(2,1)} %get-tuple-element.16.rows0, bf16[1024,512]{1,0:T(8,128)(2,1)} %get-tuple-element.12.grad0, bf16[1024,512]{1,0:T(8,128)(2,1)} %get-tuple-element.17.rows1, ...), custom_call_target="tpu_custom_call" | custom-call | flops 1073741824 | bytes 10485760 | tf_op jit(solution)/shard_map/operator_grad/pallas_call | solution.py:136
  106.3 1.7 collective-permute-start.3
  108.0 0.8 collective-permute-start.4
  109.2 3.0 %add_convert_fusion = bf16[8,4,32,512]{3,2,1,0:T(8,128)(2,1)} fusion(f32[8,4,32,512]{3,2,1,0:T(8,128)} %get-tuple-element.18, bf16[8,4,32,512]{3,2,1,0:T(8,128)(2,1)S(1)} %collective-permute-done.5), kind=kLoop, calls=%fused_computation.2 | loop fusion | flops 1572864 | bytes 4194304 | tf_op jit(solution)/shard_map/convert_element_type | solution.py:183
  112.1 5.9 %all-to-all-start.2 = ((bf16[8,4,32,512]{3,2,1,0:T(8,128)(2,1)}), bf16[8,4,32,512]{3,2,1,0:T(8,128)(2,1)S(1)}, u32[]{:S(2)}, u32[]{:S(2)}) async-start(bf16[8,4,32,512]{3,2,1,0:T(8,128)(2,1)} %add_convert_fusion), calls=%async_computation.2 | async-start | bytes 2097152 | tf_op jit(solution)/shard_map/all_to_all | solution.py:184
  118.0 0.9 constant_dynamic-slice_fusion
  118.9 8.1 %head_grad.1 = f32[1024,512]{1,0:T(8,128)} custom-call(s32[2,4]{1,0:T(2,128)} %relations.3, s32[2,1024]{1,0:T(2,128)} %head_at.1, bf16[1024,512]{1,0:T(8,128)(2,1)} %get-tuple-element.12.grad0, bf16[1024,512]{1,0:T(8,128)(2,1)} %get-tuple-element.13.grad1, bf16[4,512,512]{2,1,0:T(8,128)(2,1)} %bitcast.34), custom_call_target="tpu_custom_call" | custom-call | flops 3221225472 | bytes 6291456 | tf_op jit(solution)/shard_map/head_grad/pallas_call | solution.py:168
  127.0 14.0 %collective-permute-done.3 = bf16[1024,512]{1,0:T(8,128)(2,1)S(1)} collective-permute-done((bf16[1024,512]{1,0:T(8,128)(2,1)}, bf16[1024,512]{1,0:T(8,128)(2,1)S(1)}, u32[]{:S(2)}, u32[]{:S(2)}) %collective-permute-start.3) | collective-permute-done | bytes 1048608 | tf_op jit(solution)/shard_map/ppermute | solution.py:23
  141.0 1.0 copy-done.2
  141.9 1.0 copy-done.3
  142.9 2.1 %multiply_reduce_fusion = f32[1024]{0:T(1024)S(1)} fusion(bf16[1024,512]{1,0:T(8,128)(2,1)S(1)} %collective-permute-done.4, f32[1024,512]{1,0:T(8,128)} %head_grad.1, bf16[1024,512]{1,0:T(8,128)(2,1)S(1)} %collective-permute-done.3), kind=kLoop, calls=%fused_computation.4 | loop fusion | flops 3144704 | bytes 4198400 | tf_op jit(solution)/shard_map/reduce_sum | solution.py:216
  145.7 0.9 copy.26
  146.6 29.0 %all-to-all-start.3 = ((f32[16,32,128]{2,1,0:T(8,128)}), f32[16,32,128]{2,1,0:T(8,128)S(1)}, u32[]{:S(2)}, u32[]{:S(2)}) async-start(f32[16,32,128]{2,1,0:T(8,128)} %bitcast.14), calls=%async_computation.3 | async-start | bytes 524288 | tf_op jit(solution)/shard_map/all_to_all | solution.py:186
  175.6 4.0 %divide_subtract_fusion = f32[1024,512]{1,0:T(8,128)} fusion(f32[1024,512]{1,0:T(8,128)} %param.7, f32[1024]{0:T(1024)S(1)} %get-tuple-element.30, bf16[1024,512]{1,0:T(8,128)(2,1)} %copy-done.3, f32[1024,512]{1,0:T(8,128)S(1)} %copy-done, bf16[1024,512]{1,0:T(8,128)(2,1)} %copy-done.2), kind=kLoop, calls=%fused_computation.3 | loop fusion | flops 3670016 | bytes 8392704 | tf_op jit(solution)/shard_map/sub | solution.py:217
  179.7 8.1 %all-to-all-done.3 = f32[16,32,128]{2,1,0:T(8,128)S(1)} async-done(((f32[16,32,128]{2,1,0:T(8,128)}), f32[16,32,128]{2,1,0:T(8,128)S(1)}, u32[]{:S(2)}, u32[]{:S(2)}) %all-to-all-start.3) | async-done | bytes 262176 | tf_op jit(solution)/shard_map/all_to_all | solution.py:186
  188.1 0.6 copy.28
  (39 shorter events, 3.1 us)
Async XLA Ops:
  0.6 40.8 %copy-start.1 = (f32[1024,512]{1,0:T(8,128)S(1)}, f32[1024,512]{1,0:T(8,128)}, u32[]{:S(2)}) copy-start(f32[1024,512]{1,0:T(8,128)} %param.7) | copy-start | bytes 6291460
  41.4 2.1 %copy-start.6 = (s32[2,1024]{1,0:T(2,128)S(1)}, s32[2,1024]{1,0:T(2,128)}, u32[]{:S(2)}) copy-start(s32[2,1024]{1,0:T(2,128)} %head_at.1) | copy-start | bytes 24580
  41.4 2.2 %copy-start.5 = (s32[2,1024]{1,0:T(2,128)S(1)}, s32[2,1024]{1,0:T(2,128)}, u32[]{:S(2)}) copy-start(s32[2,1024]{1,0:T(2,128)} %param.12) | copy-start | bytes 24580
  41.4 2.2 %copy-start.7 = (s32[2,4]{1,0:T(2,128)S(1)}, s32[2,4]{1,0:T(2,128)}, u32[]{:S(2)}) copy-start(s32[2,4]{1,0:T(2,128)} %relations.3) | copy-start | bytes 100
  41.4 6.9 %collective-permute-start.1 = (bf16[8,16,16,256]{3,2,1,0:T(8,128)(2,1)S(1)}, bf16[8,16,16,256]{3,2,1,0:T(8,128)(2,1)}, u32[]{:S(2)}, u32[]{:S(2)}) collective-permute-start(bf16[8,16,16,256]{3,2,1,0:T(8,128)(2,1)S(1)} %all_to_all.21), channel_id=1, source_target_pairs={{0,16},{16,0},{32,48},{48,32},{64,80},{80,64},{96,112},{112,96},{1... | collective-permute-start | bytes 3145736 | tf_op jit(solution)/shard_map/ppermute | solution.py:23
  42.6 25.9 %collective-permute-start = (bf16[1024,512]{1,0:T(8,128)(2,1)}, bf16[1024,512]{1,0:T(8,128)(2,1)}, u32[]{:S(2)}, u32[]{:S(2)}) collective-permute-start(bf16[1024,512]{1,0:T(8,128)(2,1)} %convert_element_type.21.heads), channel_id=1, source_target_pairs={{0,1},{1,0},{2,3},{3,2},{4,5},{5,4},{6,7},{7,6},{8,9},{9,8},{10,11... | collective-permute-start | bytes 3145736 | tf_op jit(solution)/shard_map/ppermute | solution.py:23
  42.6 42.9 %collective-permute-start.2 = (bf16[1024,512]{1,0:T(8,128)(2,1)}, bf16[1024,512]{1,0:T(8,128)(2,1)S(1)}, u32[]{:S(2)}, u32[]{:S(2)}) collective-permute-start(bf16[1024,512]{1,0:T(8,128)(2,1)} %convert_element_type.21.heads), channel_id=1, source_target_pairs={{0,8},{1,9},{2,10},{3,11},{4,12},{5,13},{6,14},{7,15},{8,0},{9,1},... | collective-permute-start | bytes 3145736 | tf_op jit(solution)/shard_map/ppermute | solution.py:23
  85.5 1.0 copy-start.9
  106.3 2.9 %collective-permute-start.5 = (bf16[8,4,32,512]{3,2,1,0:T(8,128)(2,1)}, bf16[8,4,32,512]{3,2,1,0:T(8,128)(2,1)S(1)}, u32[]{:S(2)}, u32[]{:S(2)}) collective-permute-start(bf16[8,4,32,512]{3,2,1,0:T(8,128)(2,1)} %get-tuple-element.19), channel_id=1, source_target_pairs={{0,16},{16,0},{32,48},{48,32},{64,80},{80,64},{96,112},{112,96},{1... | collective-permute-start | bytes 3145736 | tf_op jit(solution)/shard_map/ppermute | solution.py:23
  106.3 34.7 %collective-permute-start.3 = (bf16[1024,512]{1,0:T(8,128)(2,1)}, bf16[1024,512]{1,0:T(8,128)(2,1)S(1)}, u32[]{:S(2)}, u32[]{:S(2)}) collective-permute-start(bf16[1024,512]{1,0:T(8,128)(2,1)} %get-tuple-element.14), channel_id=1, source_target_pairs={{0,1},{1,0},{2,3},{3,2},{4,5},{5,4},{6,7},{7,6},{8,9},{9,8},{10,11... | collective-permute-start | bytes 3145736 | tf_op jit(solution)/shard_map/ppermute | solution.py:23
  108.0 32.9 %collective-permute-start.4 = (bf16[1024,512]{1,0:T(8,128)(2,1)}, bf16[1024,512]{1,0:T(8,128)(2,1)S(1)}, u32[]{:S(2)}, u32[]{:S(2)}) collective-permute-start(bf16[1024,512]{1,0:T(8,128)(2,1)} %get-tuple-element.15), channel_id=1, source_target_pairs={{0,8},{1,9},{2,10},{3,11},{4,12},{5,13},{6,14},{7,15},{8,0},{9,1},... | collective-permute-start | bytes 3145736 | tf_op jit(solution)/shard_map/ppermute | solution.py:23
  112.1 33.5 %all-to-all-start.2 = ((bf16[8,4,32,512]{3,2,1,0:T(8,128)(2,1)}), bf16[8,4,32,512]{3,2,1,0:T(8,128)(2,1)S(1)}, u32[]{:S(2)}, u32[]{:S(2)}) async-start(bf16[8,4,32,512]{3,2,1,0:T(8,128)(2,1)} %add_convert_fusion), calls=%async_computation.2 | async-start | bytes 2097152 | tf_op jit(solution)/shard_map/all_to_all | solution.py:184
  127.0 18.0 %copy-start.8 = (f32[1024]{0:T(1024)S(1)}, f32[1024]{0:T(1024)}, u32[]{:S(2)}) copy-start(f32[1024]{0:T(1024)} %param.8) | copy-start | bytes 12292
  141.0 1.0 copy-start.2
  141.9 1.0 copy-start.3
  145.0 30.6 %copy-start = (f32[1024,512]{1,0:T(8,128)S(1)}, f32[1024,512]{1,0:T(8,128)}, u32[]{:S(2)}) copy-start(f32[1024,512]{1,0:T(8,128)} %head_grad.1) | copy-start | bytes 6291460
  146.6 41.2 %all-to-all-start.3 = ((f32[16,32,128]{2,1,0:T(8,128)}), f32[16,32,128]{2,1,0:T(8,128)S(1)}, u32[]{:S(2)}, u32[]{:S(2)}) async-start(f32[16,32,128]{2,1,0:T(8,128)} %bitcast.14), calls=%async_computation.3 | async-start | bytes 524288 | tf_op jit(solution)/shard_map/all_to_all | solution.py:186
  175.6 12.4 %copy-start.4 = (f32[4,32,32]{2,1,0:T(8,128)S(1)}, f32[4,32,32]{2,1,0:T(8,128)}, u32[]{:S(2)}) copy-start(f32[4,32,32]{2,1,0:T(8,128)} %param.10) | copy-start | bytes 49156

commit v3 on v0

v3 whole, which is shorter than its diff:
```python
import jax
import jax.numpy as jnp
from jax import lax
from jax.experimental import pallas as pl
from jax.experimental.pallas import tpu as pltpu
from jax.sharding import PartitionSpec as P


LEARN_RATE = 0.1
BF = jnp.bfloat16
F32 = jnp.float32
NN = (((1,), (0,)), ((), ()))
NT = (((1,), (1,)), ((), ()))
TN = (((0,), (0,)), ((), ()))
VMEM_BYTES = 24 << 20


def dot(a, b, dims):
    return lax.dot_general(a, b, dims, preferred_element_type=F32)


def vmem(count):
    return [pl.BlockSpec(memory_space=pltpu.VMEM)] * count


def smem(count):
    return [pl.BlockSpec(memory_space=pltpu.SMEM)] * count


def local(kernel, flops, outs, scalars, arrays, scratch=()):
    shapes = tuple(jax.ShapeDtypeStruct(*out) for out in outs)
    moved = sum(a.size * a.dtype.itemsize for a in (*arrays, *shapes))
    return pl.pallas_call(
        kernel,
        out_shape=shapes,
        in_specs=smem(len(scalars)) + vmem(len(arrays)),
        out_specs=tuple(vmem(len(shapes))),
        scratch_shapes=list(scratch),
        compiler_params=pltpu.CompilerParams(vmem_limit_bytes=VMEM_BYTES),
        cost_estimate=pl.CostEstimate(flops=flops, bytes_accessed=moved, transcendentals=0),
    )(*scalars, *arrays)


def swapped(block, axis, stride):
    count = lax.axis_size(axis)
    return lax.ppermute(block, axis, [(i, i ^ (1 << stride)) for i in range(count)])


def strided_groups(size, stride):
    return [list(range(first, size, stride)) for first in range(stride)]


def spread(piece, count, axis, groups=None):
    sent = jnp.broadcast_to(piece[None], (count, *piece.shape))
    return lax.all_to_all(sent, axis, 0, 0, axis_index_groups=groups)


def own_half_of_operators(operators):
    nrel, rows, width = operators.shape
    wide, narrow = lax.axis_size("wide"), lax.axis_size("narrow")
    place, half = lax.axis_index("wide"), width // 2
    stride = wide // nrel
    own = lax.dynamic_index_in_dim(operators, place // stride, 0, keepdims=False)
    own = lax.dynamic_slice_in_dim(own, place % 2 * half, half, 1).astype(BF)
    across = spread(own, narrow, "narrow")
    across = spread(across, nrel, "wide", strided_groups(wide, stride))
    return across.reshape(nrel, narrow * rows, half)


def picks(index, first, rows):
    spot = lax.broadcasted_iota(jnp.int32, (rows, index.shape[1]), 0) + first
    return (index == spot).astype(F32).astype(BF)


def rows_kernel(head_at, heads, rows0, rows1):
    for bucket, rows in enumerate((rows0, rows1)):
        chosen = picks(head_at[bucket : bucket + 1, :], 0, heads.shape[0])
        rows[...] = dot(chosen, heads[...], TN).astype(BF)


def halves(core, half):
    own = pl.ds(pl.multiple_of(core * half, half), half)
    other = pl.ds(pl.multiple_of((1 - core) * half, half), half)
    return own, other


def query_kernel(relations, core, rows, own, other, query):
    batches = relations.shape[0]
    edges = rows.shape[0] // batches
    first, second = halves(core[0], own.shape[2])
    for batch in range(batches):
        at = slice(batch * edges, (batch + 1) * edges)
        r = relations[batch]
        found = dot(rows[at, first], own[r], NT) + dot(rows[at, second], other[r], NT)
        query[at, :] = found.astype(BF)


def score_kernel(query, tails, tail_at, score_grad, tail_grad):
    count, edges = tails.shape[0], query.shape[0]
    parts = 4
    step = edges // parts
    for part in range(parts):
        at = slice(part * step, (part + 1) * step)
        weights = jnp.exp(dot(tails[...], query[at, :], NT))
        weights = weights * (1.0 / jnp.sum(weights, axis=0, keepdims=True))
        hit = tail_at[:, at] == lax.broadcasted_iota(jnp.int32, (count, step), 0)
        score_grad[:, at] = jnp.where(hit, weights - 1.0, weights).astype(BF)
    tail_grad[...] = dot(score_grad[...], query[...], NN).astype(BF)


def query_grad_and_sum(relations, score_grad, tails, rows, query_grad, total):
    batches = relations.shape[0]
    edges = rows.shape[0] // batches
    query_grad[...] = dot(score_grad[...], tails[...], TN).astype(BF)
    for batch in range(batches):
        at = slice(batch * edges, (batch + 1) * edges)
        part = dot(rows[at, :], query_grad[at, :], TN)
        total[relations[batch]] += part.reshape(total.shape[1:])


def first_backward_kernel(relations, score_grad, tails, rows, query_grad, total):
    total[...] = jnp.zeros_like(total)
    query_grad_and_sum(relations, score_grad, tails, rows, query_grad, total)


def last_backward_kernel(relations, core, score_grad, tails, rows, before, query_grad, kept, sent, total):
    total[...] = before[...]
    query_grad_and_sum(relations, score_grad, tails, rows, query_grad, total)
    for r in range(total.shape[0]):
        kept[:, r] = total[r, :, core[0]]
        sent[:, r] = total[r, :, 1 - core[0]].astype(BF)


def head_kernel(relations, core, head_at, grad0, grad1, own, other, total, part):
    batches = relations.shape[1]
    edges = grad0.shape[0] // batches
    parts = 4
    step = total.shape[0] // parts
    first, second = halves(core[0], own.shape[2])
    for bucket, grad in enumerate((grad0, grad1)):
        for batch in range(batches):
            at = slice(batch * edges, (batch + 1) * edges)
            r = relations[bucket, batch]
            part[at, first] = dot(grad[at, :], own[r], NN).astype(BF)
            part[at, second] = dot(grad[at, :], other[r], NN).astype(BF)
        for k in range(parts):
            to = slice(k * step, (k + 1) * step)
            added = dot(picks(head_at[bucket : bucket + 1, :], k * step, step), part[...], NN)
            if bucket == 0:
                total[to, :] = added
            else:
                total[to, :] += added


def summed_over_devices(kept, sent):
    _, nrel, columns, width = kept.shape
    narrow = lax.axis_size("narrow")
    pair = (kept + swapped(sent, "wide", 0).astype(F32)).astype(BF)
    groups = strided_groups(lax.axis_size("wide"), 2)
    got = lax.all_to_all(pair, "wide", 0, 0, axis_index_groups=groups)
    part = jnp.sum(got.astype(F32), axis=0).reshape(nrel * columns, width).T
    got = lax.all_to_all(part.reshape(narrow, width // narrow, nrel * columns), "narrow", 0, 0)
    total = jnp.sum(got, axis=0)
    return total.reshape(width // narrow, nrel, columns).transpose(1, 0, 2)


def step(entity_table, row_state, operators, op_state, head_index, tail_index, batch_relation):
    nrel, _, width = operators.shape
    count, edges = entity_table.shape[0], head_index.shape[1]
    narrow_count = lax.axis_size("narrow")
    wide_count = lax.axis_size("wide")
    flips = (0, narrow_count.bit_length() - 2)
    core = (lax.axis_index("wide") % 2).astype(jnp.int32).reshape(1)
    table_bf = entity_table.astype(BF)
    half = own_half_of_operators(operators)
    tails = [None, None]
    for bucket in (1, 0):
        tails[bucket] = swapped(table_bf, "narrow", flips[bucket])
    other = swapped(half, "wide", 0)
    flat = ((edges, width), BF)
    matmul = 2 * count * edges * width
    rows = local(rows_kernel, 2 * matmul, (flat, flat), (), (head_index, table_bf))
    score_grads, returned, query_grads = [None, None], [None, None], [None, None]
    for bucket in (0, 1):
        (query,) = local(
            query_kernel,
            matmul // 2,
            (flat,),
            (batch_relation[bucket], core),
            (rows[bucket], half, other),
        )
        score_grads[bucket], tail_grad = local(
            score_kernel,
            4 * matmul,
            (((count, edges), BF), ((count, width), BF)),
            (),
            (query, tails[bucket], tail_index[bucket : bucket + 1]),
        )
        returned[bucket] = swapped(tail_grad, "narrow", flips[bucket])
    sums = (nrel, wide_count // 2, 2, width // wide_count, width)
    query_grads[0], before = local(
        first_backward_kernel,
        2 * matmul,
        (flat, (sums, F32)),
        (batch_relation[0],),
        (score_grads[0], tails[0], rows[0]),
    )
    shares = (wide_count // 2, nrel, width // wide_count, width)
    query_grads[1], kept, sent = local(
        last_backward_kernel,
        2 * matmul,
        (flat, (shares, F32), (shares, BF)),
        (batch_relation[1], core),
        (score_grads[1], tails[1], rows[1], before),
        (pltpu.VMEM(sums, F32),),
    )
    op_shard = summed_over_devices(kept, sent)
    (head_total,) = local(
        head_kernel,
        3 * matmul,
        (((count, width), F32),),
        (batch_relation, core),
        (head_index, *query_grads, half, other),
        (pltpu.VMEM((edges, width), BF),),
    )
    entity_grad = head_total + returned[0].astype(F32) + returned[1].astype(F32)
    new_state = row_state + jnp.mean(entity_grad * entity_grad, axis=1)
    new_table = entity_table - LEARN_RATE * entity_grad / jnp.sqrt(new_state)[:, None]
    columns = width // wide_count
    first_column = lax.axis_index("wide") * columns
    own_operators = lax.dynamic_slice_in_dim(operators, first_column, columns, 2)
    new_op_state = op_state + op_shard * op_shard
    new_operators = own_operators - LEARN_RATE * op_shard / jnp.sqrt(new_op_state)
    return (new_table, new_state, new_operators, new_op_state)


def solution(mesh):
    placed = (
        P(("wide", "narrow"), None),
        P(("wide", "narrow")),
        P(None, "narrow", None),
        P(None, "narrow", "wide"),
        P(None, ("wide", "narrow")),
        P(None, ("wide", "narrow")),
        P(None, ("wide", "narrow")),
    )
    return jax.shard_map(
        step,
        mesh=mesh,
        in_specs=placed,
        out_specs=(
            P(("wide", "narrow"), None),
            P(("wide", "narrow")),
            P(None, "narrow", "wide"),
            P(None, "narrow", "wide"),
        ),
        check_vma=False,
    )
```

time: 453 us -> 171 us (0.38)
  waiting for transfers between devices: 326 us -> 41.9 us
  blocking collectives: 0 us -> 36.8 us
  matrix products: 34.6 us -> 0 us
  starting transfers between devices: 12.2 us -> 43.2 us
  Pallas kernels: 0 us -> 25.8 us
  other arithmetic: 33.5 us -> 11.1 us
  local copies, waits for them, and re-layouts: 30.5 us -> 9.17 us
  between operations: 15.4 us -> 0.91 us
    unnamed x5 -> x0, waiting for transfers between devices: 239 us -> none
    all_gather x1 -> x0, waiting for transfers between devices: 68.8 us -> none  [body(): lax.all_gather(operators.astype(jnp.bfloat16), 'narrow', axis=1, tiled=True)]
    all_to_all x0 -> x2, blocking collectives: none -> 36.8 us  [spread(): return lax.all_to_all(sent, axis, 0, 0, axis_index_groups=groups)]
    all_to_all x0 -> x2, starting transfers between devices: none -> 35.9 us  [the longest x1 28.4 us: summed_over_devices(): lax.all_to_all(part.reshape(narrow, width // narrow, nrel * columns), 'na...]
    dot_general x14 -> x0, matrix products: 34.6 us -> none  [the longest x2 6.49 us: bucket_terms(): jnp.dot(score_grad, tails_bf, preferred_element_type=jnp.float32)]
    pallas_call x0 -> x8, Pallas kernels: none -> 25.8 us  [local(): pl.pallas_call(kernel, out_shape=shapes, in_specs=smem(len(scalars)) + vm...]
    scatter-add x2 -> x0, other arithmetic: 17.6 us -> none  [bucket_terms(): jnp.zeros(heads_bf.shape, jnp.float32).at[head_rows].add(head_part)]
    gather x4 -> x0, local copies, waits for them, and re-layouts: 16.1 us -> none  [the longest x2 10.2 us: bucket_terms(): picked = heads_bf[head_rows]]
  transfers between devices with their start and end apart: 7 -> 8, of which waited for: 5 -> 5; matrix products, arithmetic and copies ran while one was open for 15% -> 6% of each run, Pallas kernels for 0% -> 10%
where the time goes in v3:
time: 171 us; the launch traced here: 169 us
  starting transfers between devices  43.2 us (25%)
  waiting for transfers between devices  41.9 us (25%)
  blocking collectives  36.8 us (22%)
  Pallas kernels  25.8 us (15%)
  other arithmetic  11.1 us (6%)
  local copies, waits for them, and re-layouts  9.17 us (5%)
    all_to_all x2, blocking collectives, spread(): return lax.all_to_all(sent, axis, 0, 0, axis_index_groups=groups)  36.8 us
    ppermute x6, waiting for transfers between devices, swapped(): lax.ppermute(block, axis, [(i, i ^ 1 << stride) for i in range(count)])  31.8 us
    all_to_all x1, starting transfers between devices, summed_over_devices(): lax.all_to_all(part.reshape(narrow, width // narrow, nrel * columns), 'na...  28.4 us
    pallas_call x8, Pallas kernels, local(): pl.pallas_call(kernel, out_shape=shapes, in_specs=smem(len(scalars)) + vm...  25.8 us
    all_to_all x1, waiting for transfers between devices, summed_over_devices(): lax.all_to_all(part.reshape(narrow, width // narrow, nrel * columns), 'na...  8.06 us
    unnamed x28, local copies, waits for them, and re-layouts  7.83 us
    all_to_all x1, starting transfers between devices, summed_over_devices(): got = lax.all_to_all(pair, 'wide', 0, 0, axis_index_groups=groups)  7.49 us
    ppermute x6, starting transfers between devices, swapped(): lax.ppermute(block, axis, [(i, i ^ 1 << stride) for i in range(count)])  7.37 us
  transfers between devices with their start and end apart: 8, of which 5 were waited for; matrix products, arithmetic and copies ran while one was open for 6% of the time, Pallas kernels for 10%

profile of v3, /device:TPU:4, one launch (start us, length us, event | category | flops | bytes accessed | tf_op | source)
XLA Modules:
  0.0 168.8 jit_solution(6631894166069065244)
XLA Ops:
  0.7 0.9 copy-done
  1.7 21.5 %all_to_all.20 = bf16[16,32,256]{2,1,0:T(8,128)(2,1)S(1)} all-to-all(bf16[16,32,256]{2,1,0:T(8,128)(2,1)S(1)} %broadcast_in_dim.7), channel_id=1, replica_groups=mesh['wide'=16,'narrow'=16] {'narrow'}, dimensions={0} | all-to-all | bytes 524288 | tf_op jit(solution)/shard_map/all_to_all | solution.py:55
  23.3 15.3 %all_to_all.21 = bf16[4,16,32,256]{3,2,1,0:T(8,128)(2,1)S(1)} all-to-all(bf16[4,16,32,256]{3,2,1,0:T(8,128)(2,1)S(1)} %broadcast_in_dim.8), channel_id=1, replica_groups={{0,64,128,192},{16,80,144,208},{32,96,160,224},{48,112,176,240},{1,65,1..., dimensions={0} | all-to-all | bytes 2097152 | tf_op jit(solution)/shard_map/all_to_all | solution.py:55
  39.3 2.3 %collective-permute-start.2 = (bf16[1024,512]{1,0:T(8,128)(2,1)S(1)}, bf16[1024,512]{1,0:T(8,128)(2,1)S(1)}, u32[]{:S(2)}, u32[]{:S(2)}) collective-permute-start(bf16[1024,512]{1,0:T(8,128)(2,1)S(1)} %convert_element_type.22.heads), channel_id=1, source_target_pairs={{0,8},{1,9},{2,10},{3,11},{4,12},{5,13},{6,14},{7,15},{8,0},{9,1},... | collective-permute-start | bytes 3145736 | tf_op jit(solution)/shard_map/ppermute | solution.py:46
  41.6 2.4 %shard_map.102 = (bf16[1024,512]{1,0:T(8,128)(2,1)S(1)}, bf16[1024,512]{1,0:T(8,128)(2,1)S(1)}) custom-call(s32[2,1024]{1,0:T(2,128)S(1)} %copy-done.6, bf16[1024,512]{1,0:T(8,128)(2,1)S(1)} %convert_element_type.22.heads), custom_call_target="tpu_custom_call" | custom-call | flops 2147483648 | bytes 3153920 | tf_op jit(solution)/shard_map/pallas_call | solution.py:33
  44.1 1.3 shard_map.103.query
  45.4 1.3 shard_map.106.query
  46.7 17.7 %collective-permute-done.1.tails = bf16[1024,512]{1,0:T(8,128)(2,1)S(1)} collective-permute-done((bf16[1024,512]{1,0:T(8,128)(2,1)S(1)}, bf16[1024,512]{1,0:T(8,128)(2,1)S(1)}, u32[]{:S(2)}, u32[]{:S(2)}) %collective-permute-start.1) | collective-permute-done | bytes 1048608 | tf_op jit(solution)/shard_map/ppermute | solution.py:46
  64.4 4.8 %shard_map.104 = (bf16[1024,1024]{1,0:T(8,128)(2,1)S(1)}, bf16[1024,512]{1,0:T(8,128)(2,1)}) custom-call(bf16[1024,512]{1,0:T(8,128)(2,1)S(1)} %shard_map.103.query, bf16[1024,512]{1,0:T(8,128)(2,1)S(1)} %collective-permute-done.1.tails, s32[1,1024]{1,0:T(1,128)S(1)} %get-tuple-element.40.tail_at), custom_call_target="tpu_custom_call" | custom-call | flops 4294967296 | bytes 5246976 | tf_op jit(solution)/shard_map/pallas_call | solution.py:33
  69.2 2.7 %shard_map.105 = (bf16[1024,512]{1,0:T(8,128)(2,1)S(1)}, f32[4,8,2,32,512]{4,3,2,1,0:T(8,128)S(1)}) custom-call(s32[4]{0:T(128)S(1)} %get-tuple-element.42.relations, bf16[1024,1024]{1,0:T(8,128)(2,1)S(1)} %get-tuple-element.16.score_grad, bf16[1024,512]{1,0:T(8,128)(2,1)S(1)} %collective-permute-done.1.tails, bf16[1024,512]{1,0:T(8,128)(2,1)S(1)} %get-tuple-element.15.rows), custom_call_target="tpu_custom_call" | custom-call | flops 2147483648 | bytes 9437184 | tf_op jit(solution)/shard_map/pallas_call | solution.py:33
  72.0 1.0 copy-done.7
  72.9 2.0 %collective-permute-done.2.tails = bf16[1024,512]{1,0:T(8,128)(2,1)S(1)} collective-permute-done((bf16[1024,512]{1,0:T(8,128)(2,1)S(1)}, bf16[1024,512]{1,0:T(8,128)(2,1)S(1)}, u32[]{:S(2)}, u32[]{:S(2)}) %collective-permute-start.2) | collective-permute-done | bytes 1048608 | tf_op jit(solution)/shard_map/ppermute | solution.py:46
  75.0 4.8 %shard_map.107 = (bf16[1024,1024]{1,0:T(8,128)(2,1)S(1)}, bf16[1024,512]{1,0:T(8,128)(2,1)}) custom-call(bf16[1024,512]{1,0:T(8,128)(2,1)S(1)} %shard_map.106.query, bf16[1024,512]{1,0:T(8,128)(2,1)S(1)} %collective-permute-done.2.tails, s32[1,1024]{1,0:T(1,128)S(1)} %get-tuple-element.41.tail_at), custom_call_target="tpu_custom_call" | custom-call | flops 4294967296 | bytes 5246976 | tf_op jit(solution)/shard_map/pallas_call | solution.py:33
  79.8 4.2 %shard_map.108 = (bf16[1024,512]{1,0:T(8,128)(2,1)S(1)}, f32[8,4,32,512]{3,2,1,0:T(8,128)S(1)}, bf16[8,4,32,512]{3,2,1,0:T(8,128)(2,1)}) custom-call(s32[4]{0:T(128)S(1)} %get-tuple-element.43.relations, s32[1]{0:T(128)} %bitcast.core, bf16[1024,1024]{1,0:T(8,128)(2,1)S(1)} %get-tuple-element.19.score_grad, ...), custom_call_target="tpu_custom_call" | custom-call | flops 2147483648 | bytes 12582912 | tf_op jit(solution)/shard_map/pallas_call | solution.py:33
  83.9 1.0 copy-done.4
  84.9 1.5 collective-permute-start.3
  86.4 3.0 %collective-permute-start.4 = (bf16[1024,512]{1,0:T(8,128)(2,1)}, bf16[1024,512]{1,0:T(8,128)(2,1)}, u32[]{:S(2)}, u32[]{:S(2)}) collective-permute-start(bf16[1024,512]{1,0:T(8,128)(2,1)} %get-tuple-element.23), channel_id=1, source_target_pairs={{0,8},{1,9},{2,10},{3,11},{4,12},{5,13},{6,14},{7,15},{8,0},{9,1},... | collective-permute-start | bytes 3145736 | tf_op jit(solution)/shard_map/ppermute | solution.py:46
  89.4 2.6 %add_convert_fusion = bf16[8,4,32,512]{3,2,1,0:T(8,128)(2,1)} fusion(f32[8,4,32,512]{3,2,1,0:T(8,128)S(1)} %get-tuple-element.24, bf16[8,4,32,512]{3,2,1,0:T(8,128)(2,1)} %collective-permute-done.5), kind=kLoop, calls=%fused_computation.1 | loop fusion | flops 1572864 | bytes 4194304 | tf_op jit(solution)/shard_map/convert_element_type | solution.py:158
  92.1 7.5 %all-to-all-start.2 = ((bf16[8,4,32,512]{3,2,1,0:T(8,128)(2,1)}), bf16[8,4,32,512]{3,2,1,0:T(8,128)(2,1)}, u32[]{:S(2)}, u32[]{:S(2)}) async-start(bf16[8,4,32,512]{3,2,1,0:T(8,128)(2,1)} %add_convert_fusion), calls=%async_computation.2 | async-start | bytes 2097152 | tf_op jit(solution)/shard_map/all_to_all | solution.py:160
  99.6 1.2 copy-done.2
  100.9 1.2 copy-done.5
  102.1 1.2 copy-done.8
  103.3 4.3 %shard_map.109 = f32[1024,512]{1,0:T(8,128)S(1)} custom-call(s32[2,4]{1,0:T(2,128)S(1)} %copy-done.3, s32[1]{0:T(128)} %bitcast.core, s32[2,1024]{1,0:T(2,128)S(1)} %copy-done.6, bf16[1024,512]{1,0:T(8,128)(2,1)S(1)} %copy-done.8, bf16[1024,512]{1,0:T(8,128)(2,1)S(1)} %copy-done.5, bf16[4,512,256]{2,1,0:T(8,128)(2,1)S(1)} %bitcast.22, ...), custom_call_target="tpu_custom_call" | custom-call | flops 3221225472 | bytes 6299648 | tf_op jit(solution)/shard_map/pallas_call | solution.py:33
  107.7 12.0 %collective-permute-done.3 = bf16[1024,512]{1,0:T(8,128)(2,1)} collective-permute-done((bf16[1024,512]{1,0:T(8,128)(2,1)}, bf16[1024,512]{1,0:T(8,128)(2,1)}, u32[]{:S(2)}, u32[]{:S(2)}) %collective-permute-start.3) | collective-permute-done | bytes 1048608 | tf_op jit(solution)/shard_map/ppermute | solution.py:46
  119.7 2.1 %multiply_reduce_fusion = f32[1024]{0:T(1024)S(1)} fusion(bf16[1024,512]{1,0:T(8,128)(2,1)} %collective-permute-done.4, f32[1024,512]{1,0:T(8,128)S(1)} %shard_map.109, bf16[1024,512]{1,0:T(8,128)(2,1)} %collective-permute-done.3), kind=kLoop, calls=%fused_computation.3 | loop fusion | flops 3144704 | bytes 4198400 | tf_op jit(solution)/shard_map/reduce_sum | solution.py:227
  122.4 2.0 %all-to-all-done.2 = bf16[8,4,32,512]{3,2,1,0:T(8,128)(2,1)} async-done(((bf16[8,4,32,512]{3,2,1,0:T(8,128)(2,1)}), bf16[8,4,32,512]{3,2,1,0:T(8,128)(2,1)}, u32[]{:S(2)}, u32[]{:S(2)}) %all-to-all-start.2) | async-done | bytes 1048608 | tf_op jit(solution)/shard_map/all_to_all | solution.py:160
  124.4 1.4 convert_reduce_fusion
  125.8 0.8 copy.16
  126.6 28.4 %all-to-all-start.3 = ((f32[16,32,128]{2,1,0:T(8,128)}), f32[16,32,128]{2,1,0:T(8,128)S(1)}, u32[]{:S(2)}, u32[]{:S(2)}) async-start(f32[16,32,128]{2,1,0:T(8,128)} %bitcast.7), calls=%async_computation.3 | async-start | bytes 524288 | tf_op jit(solution)/shard_map/all_to_all | solution.py:162
  155.0 4.1 %divide_subtract_fusion = f32[1024,512]{1,0:T(8,128)} fusion(f32[1024,512]{1,0:T(8,128)} %param.7, f32[1024]{0:T(1024)S(1)} %get-tuple-element.36, bf16[1024,512]{1,0:T(8,128)(2,1)} %collective-permute-done.4, f32[1024,512]{1,0:T(8,128)S(1)} %shard_map.109, bf16[1024,512]{1,0:T(8,128)(2,1)} %collective-permute-done.3), kind=kLoop, calls=%fused_computation.2 | loop fusion | flops 3670016 | bytes 8392704 | tf_op jit(solution)/shard_map/sub | solution.py:228
  159.1 8.1 %all-to-all-done.3 = f32[16,32,128]{2,1,0:T(8,128)S(1)} async-done(((f32[16,32,128]{2,1,0:T(8,128)}), f32[16,32,128]{2,1,0:T(8,128)S(1)}, u32[]{:S(2)}, u32[]{:S(2)}) %all-to-all-start.3) | async-done | bytes 262176 | tf_op jit(solution)/shard_map/all_to_all | solution.py:162
  167.5 0.6 copy.18
  (40 shorter events, 2.6 us)
Async XLA Ops:
  0.6 1.0 copy-start
  1.7 37.0 %copy-start.9 = (f32[1024,512]{1,0:T(8,128)S(1)}, f32[1024,512]{1,0:T(8,128)}, u32[]{:S(2)}) copy-start(f32[1024,512]{1,0:T(8,128)} %param.7) | copy-start | bytes 6291460
  38.6 3.0 %copy-start.3 = (s32[2,4]{1,0:T(2,128)S(1)}, s32[2,4]{1,0:T(2,128)}, u32[]{:S(2)}) copy-start(s32[2,4]{1,0:T(2,128)} %relations.1) | copy-start | bytes 100
  38.6 3.0 %copy-start.6 = (s32[2,1024]{1,0:T(2,128)S(1)}, s32[2,1024]{1,0:T(2,128)}, u32[]{:S(2)}) copy-start(s32[2,1024]{1,0:T(2,128)} %head_at.3) | copy-start | bytes 24580
  38.6 5.4 %collective-permute-start = (bf16[4,512,256]{2,1,0:T(8,128)(2,1)S(1)}, bf16[4,512,256]{2,1,0:T(8,128)(2,1)S(1)}, u32[]{:S(2)}, u32[]{:S(2)}) collective-permute-start(bf16[4,512,256]{2,1,0:T(8,128)(2,1)S(1)} %bitcast.19), channel_id=1, source_target_pairs={{0,16},{16,0},{32,48},{48,32},{64,80},{80,64},{96,112},{112,96},{1... | collective-permute-start | bytes 3145736 | tf_op jit(solution)/shard_map/ppermute | solution.py:46
  38.8 25.6 %collective-permute-start.1 = (bf16[1024,512]{1,0:T(8,128)(2,1)S(1)}, bf16[1024,512]{1,0:T(8,128)(2,1)S(1)}, u32[]{:S(2)}, u32[]{:S(2)}) collective-permute-start(bf16[1024,512]{1,0:T(8,128)(2,1)S(1)} %convert_element_type.22.heads), channel_id=1, source_target_pairs={{0,1},{1,0},{2,3},{3,2},{4,5},{5,4},{6,7},{7,6},{8,9},{9,8},{10,11... | collective-permute-start | bytes 3145736 | tf_op jit(solution)/shard_map/ppermute | solution.py:46
  39.3 35.6 %collective-permute-start.2 = (bf16[1024,512]{1,0:T(8,128)(2,1)S(1)}, bf16[1024,512]{1,0:T(8,128)(2,1)S(1)}, u32[]{:S(2)}, u32[]{:S(2)}) collective-permute-start(bf16[1024,512]{1,0:T(8,128)(2,1)S(1)} %convert_element_type.22.heads), channel_id=1, source_target_pairs={{0,8},{1,9},{2,10},{3,11},{4,12},{5,13},{6,14},{7,15},{8,0},{9,1},... | collective-permute-start | bytes 3145736 | tf_op jit(solution)/shard_map/ppermute | solution.py:46
  41.6 2.4 %copy-start.11 = (s32[2,1024]{1,0:T(2,128)S(1)}, s32[2,1024]{1,0:T(2,128)}, u32[]{:S(2)}) copy-start(s32[2,1024]{1,0:T(2,128)} %param.12) | copy-start | bytes 24580
  44.1 1.3 copy-start.1
  71.9 1.0 copy-start.7
  83.9 1.0 copy-start.4
  84.9 4.5 %collective-permute-start.5 = (bf16[8,4,32,512]{3,2,1,0:T(8,128)(2,1)}, bf16[8,4,32,512]{3,2,1,0:T(8,128)(2,1)}, u32[]{:S(2)}, u32[]{:S(2)}) collective-permute-start(bf16[8,4,32,512]{3,2,1,0:T(8,128)(2,1)} %get-tuple-element.25), channel_id=1, source_target_pairs={{0,16},{16,0},{32,48},{48,32},{64,80},{80,64},{96,112},{112,96},{1... | collective-permute-start | bytes 3145736 | tf_op jit(solution)/shard_map/ppermute | solution.py:46
  84.9 34.8 %collective-permute-start.3 = (bf16[1024,512]{1,0:T(8,128)(2,1)}, bf16[1024,512]{1,0:T(8,128)(2,1)}, u32[]{:S(2)}, u32[]{:S(2)}) collective-permute-start(bf16[1024,512]{1,0:T(8,128)(2,1)} %get-tuple-element.22), channel_id=1, source_target_pairs={{0,1},{1,0},{2,3},{3,2},{4,5},{5,4},{6,7},{7,6},{8,9},{9,8},{10,11... | collective-permute-start | bytes 3145736 | tf_op jit(solution)/shard_map/ppermute | solution.py:46
  86.4 33.3 %collective-permute-start.4 = (bf16[1024,512]{1,0:T(8,128)(2,1)}, bf16[1024,512]{1,0:T(8,128)(2,1)}, u32[]{:S(2)}, u32[]{:S(2)}) collective-permute-start(bf16[1024,512]{1,0:T(8,128)(2,1)} %get-tuple-element.23), channel_id=1, source_target_pairs={{0,8},{1,9},{2,10},{3,11},{4,12},{5,13},{6,14},{7,15},{8,0},{9,1},... | collective-permute-start | bytes 3145736 | tf_op jit(solution)/shard_map/ppermute | solution.py:46
  92.1 32.3 %all-to-all-start.2 = ((bf16[8,4,32,512]{3,2,1,0:T(8,128)(2,1)}), bf16[8,4,32,512]{3,2,1,0:T(8,128)(2,1)}, u32[]{:S(2)}, u32[]{:S(2)}) async-start(bf16[8,4,32,512]{3,2,1,0:T(8,128)(2,1)} %add_convert_fusion), calls=%async_computation.2 | async-start | bytes 2097152 | tf_op jit(solution)/shard_map/all_to_all | solution.py:160
  99.6 1.2 copy-start.2
  100.9 1.2 copy-start.5
  102.1 1.2 copy-start.8
  107.7 14.1 %copy-start.12 = (f32[1024]{0:T(1024)S(1)}, f32[1024]{0:T(1024)}, u32[]{:S(2)}) copy-start(f32[1024]{0:T(1024)} %param.8) | copy-start | bytes 12292
  126.6 40.6 %all-to-all-start.3 = ((f32[16,32,128]{2,1,0:T(8,128)}), f32[16,32,128]{2,1,0:T(8,128)S(1)}, u32[]{:S(2)}, u32[]{:S(2)}) async-start(f32[16,32,128]{2,1,0:T(8,128)} %bitcast.7), calls=%async_computation.3 | async-start | bytes 524288 | tf_op jit(solution)/shard_map/all_to_all | solution.py:162
  155.0 12.4 %copy-start.10 = (f32[4,32,32]{2,1,0:T(8,128)S(1)}, f32[4,32,32]{2,1,0:T(8,128)}, u32[]{:S(2)}) copy-start(f32[4,32,32]{2,1,0:T(8,128)} %param.10) | copy-start | bytes 49156

commit v4 on v3

--- a/solution.py
+++ b/solution.py
@@ -152,6 +152,18 @@
                 total[to, :] += added
 
 
+def op_update_kernel(got, state, operators, new_operators, new_state):
+    total = got[0].astype(F32)
+    for source in range(1, got.shape[0]):
+        total += got[source].astype(F32)
+    columns = state.shape[2]
+    for r in range(state.shape[0]):
+        grad = total[:, r * columns : (r + 1) * columns]
+        sums = state[r] + grad * grad
+        new_state[r] = sums
+        new_operators[r] = operators[r] - LEARN_RATE * grad / jnp.sqrt(sums)
+
+
 def summed_over_devices(kept, sent):
     _, nrel, columns, width = kept.shape
     narrow = lax.axis_size("narrow")
@@ -159,9 +171,8 @@
     groups = strided_groups(lax.axis_size("wide"), 2)
     got = lax.all_to_all(pair, "wide", 0, 0, axis_index_groups=groups)
     part = jnp.sum(got.astype(F32), axis=0).reshape(nrel * columns, width).T
-    got = lax.all_to_all(part.reshape(narrow, width // narrow, nrel * columns), "narrow", 0, 0)
-    total = jnp.sum(got, axis=0)
-    return total.reshape(width // narrow, nrel, columns).transpose(1, 0, 2)
+    part = part.astype(BF).reshape(narrow, width // narrow, nrel * columns)
+    return lax.all_to_all(part, "narrow", 0, 0)
 
 
 def step(entity_table, row_state, operators, op_state, head_index, tail_index, batch_relation):
@@ -214,7 +225,7 @@
         (score_grads[1], tails[1], rows[1], before),
         (pltpu.VMEM(sums, F32),),
     )
-    op_shard = summed_over_devices(kept, sent)
+    op_parts = summed_over_devices(kept, sent)
     (head_total,) = local(
         head_kernel,
         3 * matmul,
@@ -229,8 +240,10 @@
     columns = width // wide_count
     first_column = lax.axis_index("wide") * columns
     own_operators = lax.dynamic_slice_in_dim(operators, first_column, columns, 2)
-    new_op_state = op_state + op_shard * op_shard
-    new_operators = own_operators - LEARN_RATE * op_shard / jnp.sqrt(new_op_state)
+    share = (op_state.shape, F32)
+    new_operators, new_op_state = local(
+        op_update_kernel, 8 * op_state.size, (share, share), (), (op_parts, op_state, own_operators)
+    )
     return (new_table, new_state, new_operators, new_op_state)
 
 

time: 171 us -> 168 us (0.982)
  waiting for transfers between devices: 41.9 us -> 39.5 us
    all_to_all x1, waiting for transfers between devices: 8.06 us -> 5.7 us  [summed_over_devices(): return lax.all_to_all(part, 'narrow', 0, 0)]
    unnamed x28 -> x26, local copies, waits for them, and re-layouts: 7.83 us -> 6.54 us
    pallas_call x8 -> x9, Pallas kernels: 25.8 us -> 26.7 us  [local(): pl.pallas_call(kernel, out_shape=shapes, in_specs=smem(len(scalars)) + vm...]
where the time goes in v4:
time: 168 us; the launch traced here: 166 us
  starting transfers between devices  43.2 us (26%)
  waiting for transfers between devices  39.5 us (24%)
  blocking collectives  36.8 us (22%)
  Pallas kernels  26.7 us (16%)
  other arithmetic  10.9 us (6%)
  local copies, waits for them, and re-layouts  7.61 us (5%)
    all_to_all x2, blocking collectives, spread(): return lax.all_to_all(sent, axis, 0, 0, axis_index_groups=groups)  36.8 us
    ppermute x6, waiting for transfers between devices, swapped(): lax.ppermute(block, axis, [(i, i ^ 1 << stride) for i in range(count)])  31.8 us
    all_to_all x1, starting transfers between devices, summed_over_devices(): return lax.all_to_all(part, 'narrow', 0, 0)  28.4 us
    pallas_call x9, Pallas kernels, local(): pl.pallas_call(kernel, out_shape=shapes, in_specs=smem(len(scalars)) + vm...  26.7 us
    all_to_all x1, starting transfers between devices, summed_over_devices(): got = lax.all_to_all(pair, 'wide', 0, 0, axis_index_groups=groups)  7.49 us
    ppermute x6, starting transfers between devices, swapped(): lax.ppermute(block, axis, [(i, i ^ 1 << stride) for i in range(count)])  7.37 us
    unnamed x26, local copies, waits for them, and re-layouts  6.54 us
    all_to_all x1, waiting for transfers between devices, summed_over_devices(): return lax.all_to_all(part, 'narrow', 0, 0)  5.7 us
  transfers between devices with their start and end apart: 8, of which 5 were waited for; matrix products, arithmetic and copies ran while one was open for 6% of the time, Pallas kernels for 10%

profile of v4, /device:TPU:4, one launch (start us, length us, event | category | flops | bytes accessed | tf_op | source)
XLA Modules:
  0.0 165.6 jit_solution(16491795518889127302)
XLA Ops:
  0.7 0.9 copy-done
  1.7 21.5 %all_to_all.20 = bf16[16,32,256]{2,1,0:T(8,128)(2,1)S(1)} all-to-all(bf16[16,32,256]{2,1,0:T(8,128)(2,1)S(1)} %broadcast_in_dim.7), channel_id=1, replica_groups=mesh['wide'=16,'narrow'=16] {'narrow'}, dimensions={0} | all-to-all | bytes 524288 | tf_op jit(solution)/shard_map/all_to_all | solution.py:55
  23.3 15.3 %all_to_all.21 = bf16[4,16,32,256]{3,2,1,0:T(8,128)(2,1)S(1)} all-to-all(bf16[4,16,32,256]{3,2,1,0:T(8,128)(2,1)S(1)} %broadcast_in_dim.8), channel_id=1, replica_groups={{0,64,128,192},{16,80,144,208},{32,96,160,224},{48,112,176,240},{1,65,1..., dimensions={0} | all-to-all | bytes 2097152 | tf_op jit(solution)/shard_map/all_to_all | solution.py:55
  39.3 2.3 %collective-permute-start.2 = (bf16[1024,512]{1,0:T(8,128)(2,1)S(1)}, bf16[1024,512]{1,0:T(8,128)(2,1)S(1)}, u32[]{:S(2)}, u32[]{:S(2)}) collective-permute-start(bf16[1024,512]{1,0:T(8,128)(2,1)S(1)} %convert_element_type.27.heads), channel_id=1, source_target_pairs={{0,8},{1,9},{2,10},{3,11},{4,12},{5,13},{6,14},{7,15},{8,0},{9,1},... | collective-permute-start | bytes 3145736 | tf_op jit(solution)/shard_map/ppermute | solution.py:46
  41.6 2.4 %shard_map.102 = (bf16[1024,512]{1,0:T(8,128)(2,1)S(1)}, bf16[1024,512]{1,0:T(8,128)(2,1)S(1)}) custom-call(s32[2,1024]{1,0:T(2,128)S(1)} %copy-done.7, bf16[1024,512]{1,0:T(8,128)(2,1)S(1)} %convert_element_type.27.heads), custom_call_target="tpu_custom_call" | custom-call | flops 2147483648 | bytes 3153920 | tf_op jit(solution)/shard_map/pallas_call | solution.py:33
  44.1 1.3 shard_map.103.query
  45.4 1.3 shard_map.106.query
  46.7 17.8 %collective-permute-done.1.tails = bf16[1024,512]{1,0:T(8,128)(2,1)S(1)} collective-permute-done((bf16[1024,512]{1,0:T(8,128)(2,1)S(1)}, bf16[1024,512]{1,0:T(8,128)(2,1)S(1)}, u32[]{:S(2)}, u32[]{:S(2)}) %collective-permute-start.1) | collective-permute-done | bytes 1048608 | tf_op jit(solution)/shard_map/ppermute | solution.py:46
  64.4 4.8 %shard_map.104 = (bf16[1024,1024]{1,0:T(8,128)(2,1)S(1)}, bf16[1024,512]{1,0:T(8,128)(2,1)}) custom-call(bf16[1024,512]{1,0:T(8,128)(2,1)S(1)} %shard_map.103.query, bf16[1024,512]{1,0:T(8,128)(2,1)S(1)} %collective-permute-done.1.tails, s32[1,1024]{1,0:T(1,128)S(1)} %get-tuple-element.32.tail_at), custom_call_target="tpu_custom_call" | custom-call | flops 4294967296 | bytes 5246976 | tf_op jit(solution)/shard_map/pallas_call | solution.py:33
  69.3 2.7 %shard_map.105 = (bf16[1024,512]{1,0:T(8,128)(2,1)S(1)}, f32[4,8,2,32,512]{4,3,2,1,0:T(8,128)S(1)}) custom-call(s32[4]{0:T(128)S(1)} %get-tuple-element.34.relations, bf16[1024,1024]{1,0:T(8,128)(2,1)S(1)} %get-tuple-element.18.score_grad, bf16[1024,512]{1,0:T(8,128)(2,1)S(1)} %collective-permute-done.1.tails, bf16[1024,512]{1,0:T(8,128)(2,1)S(1)} %get-tuple-element.17.rows), custom_call_target="tpu_custom_call" | custom-call | flops 2147483648 | bytes 9437184 | tf_op jit(solution)/shard_map/pallas_call | solution.py:33
  72.0 0.9 copy-done.8
  72.9 2.0 %collective-permute-done.2.tails = bf16[1024,512]{1,0:T(8,128)(2,1)S(1)} collective-permute-done((bf16[1024,512]{1,0:T(8,128)(2,1)S(1)}, bf16[1024,512]{1,0:T(8,128)(2,1)S(1)}, u32[]{:S(2)}, u32[]{:S(2)}) %collective-permute-start.2) | collective-permute-done | bytes 1048608 | tf_op jit(solution)/shard_map/ppermute | solution.py:46
  75.0 4.8 %shard_map.107 = (bf16[1024,1024]{1,0:T(8,128)(2,1)S(1)}, bf16[1024,512]{1,0:T(8,128)(2,1)}) custom-call(bf16[1024,512]{1,0:T(8,128)(2,1)S(1)} %shard_map.106.query, bf16[1024,512]{1,0:T(8,128)(2,1)S(1)} %collective-permute-done.2.tails, s32[1,1024]{1,0:T(1,128)S(1)} %get-tuple-element.33.tail_at), custom_call_target="tpu_custom_call" | custom-call | flops 4294967296 | bytes 5246976 | tf_op jit(solution)/shard_map/pallas_call | solution.py:33
  79.8 4.1 %shard_map.108 = (bf16[1024,512]{1,0:T(8,128)(2,1)S(1)}, f32[8,4,32,512]{3,2,1,0:T(8,128)S(1)}, bf16[8,4,32,512]{3,2,1,0:T(8,128)(2,1)}) custom-call(s32[4]{0:T(128)S(1)} %get-tuple-element.35.relations, s32[1]{0:T(128)} %bitcast.core, bf16[1024,1024]{1,0:T(8,128)(2,1)S(1)} %get-tuple-element.21.score_grad, ...), custom_call_target="tpu_custom_call" | custom-call | flops 2147483648 | bytes 12582912 | tf_op jit(solution)/shard_map/pallas_call | solution.py:33
  83.9 1.0 copy-done.5
  84.9 1.5 collective-permute-start.3
  86.4 3.0 %collective-permute-start.4 = (bf16[1024,512]{1,0:T(8,128)(2,1)}, bf16[1024,512]{1,0:T(8,128)(2,1)}, u32[]{:S(2)}, u32[]{:S(2)}) collective-permute-start(bf16[1024,512]{1,0:T(8,128)(2,1)} %get-tuple-element.25), channel_id=1, source_target_pairs={{0,8},{1,9},{2,10},{3,11},{4,12},{5,13},{6,14},{7,15},{8,0},{9,1},... | collective-permute-start | bytes 3145736 | tf_op jit(solution)/shard_map/ppermute | solution.py:46
  89.4 2.6 %add_convert_fusion = bf16[8,4,32,512]{3,2,1,0:T(8,128)(2,1)} fusion(f32[8,4,32,512]{3,2,1,0:T(8,128)S(1)} %get-tuple-element.26, bf16[8,4,32,512]{3,2,1,0:T(8,128)(2,1)} %collective-permute-done.5), kind=kLoop, calls=%fused_computation | loop fusion | flops 1572864 | bytes 4194304 | tf_op jit(solution)/shard_map/convert_element_type | solution.py:170
  92.0 7.5 %all-to-all-start.2 = ((bf16[8,4,32,512]{3,2,1,0:T(8,128)(2,1)}), bf16[8,4,32,512]{3,2,1,0:T(8,128)(2,1)}, u32[]{:S(2)}, u32[]{:S(2)}) async-start(bf16[8,4,32,512]{3,2,1,0:T(8,128)(2,1)} %add_convert_fusion), calls=%async_computation.2 | async-start | bytes 2097152 | tf_op jit(solution)/shard_map/all_to_all | solution.py:172
  99.6 1.2 copy-done.2
  100.8 1.2 copy-done.6
  102.1 1.2 copy-done.9
  103.3 4.3 %shard_map.109 = f32[1024,512]{1,0:T(8,128)S(1)} custom-call(s32[2,4]{1,0:T(2,128)S(1)} %copy-done.4, s32[1]{0:T(128)} %bitcast.core, s32[2,1024]{1,0:T(2,128)S(1)} %copy-done.7, bf16[1024,512]{1,0:T(8,128)(2,1)S(1)} %copy-done.9, bf16[1024,512]{1,0:T(8,128)(2,1)S(1)} %copy-done.6, bf16[4,512,256]{2,1,0:T(8,128)(2,1)S(1)} %bitcast.15, ...), custom_call_target="tpu_custom_call" | custom-call | flops 3221225472 | bytes 6299648 | tf_op jit(solution)/shard_map/pallas_call | solution.py:33
  107.6 12.0 %collective-permute-done.3 = bf16[1024,512]{1,0:T(8,128)(2,1)} collective-permute-done((bf16[1024,512]{1,0:T(8,128)(2,1)}, bf16[1024,512]{1,0:T(8,128)(2,1)}, u32[]{:S(2)}, u32[]{:S(2)}) %collective-permute-start.3) | collective-permute-done | bytes 1048608 | tf_op jit(solution)/shard_map/ppermute | solution.py:46
  119.7 2.1 %multiply_reduce_fusion = f32[1024]{0:T(1024)S(1)} fusion(bf16[1024,512]{1,0:T(8,128)(2,1)} %collective-permute-done.4, f32[1024,512]{1,0:T(8,128)S(1)} %shard_map.109, bf16[1024,512]{1,0:T(8,128)(2,1)} %collective-permute-done.3), kind=kLoop, calls=%fused_computation.2 | loop fusion | flops 3144704 | bytes 4198400 | tf_op jit(solution)/shard_map/reduce_sum | solution.py:238
  122.3 2.0 %all-to-all-done.2 = bf16[8,4,32,512]{3,2,1,0:T(8,128)(2,1)} async-done(((bf16[8,4,32,512]{3,2,1,0:T(8,128)(2,1)}), bf16[8,4,32,512]{3,2,1,0:T(8,128)(2,1)}, u32[]{:S(2)}, u32[]{:S(2)}) %all-to-all-start.2) | async-done | bytes 1048608 | tf_op jit(solution)/shard_map/all_to_all | solution.py:172
  124.4 1.4 reduce_sum.22
  125.7 0.8 copy.11
  126.5 28.4 %all-to-all-start.3 = ((bf16[16,32,128]{2,1,0:T(8,128)(2,1)}), bf16[16,32,128]{2,1,0:T(8,128)(2,1)S(1)}, u32[]{:S(2)}, u32[]{:S(2)}) async-start(bf16[16,32,128]{2,1,0:T(8,128)(2,1)} %bitcast.7), calls=%async_computation.3 | async-start | bytes 262144 | tf_op jit(solution)/shard_map/all_to_all | solution.py:175
  154.9 4.1 %divide_subtract_fusion = f32[1024,512]{1,0:T(8,128)} fusion(f32[1024,512]{1,0:T(8,128)} %param.7, f32[1024]{0:T(1024)S(1)} %get-tuple-element.30, bf16[1024,512]{1,0:T(8,128)(2,1)} %collective-permute-done.4, f32[1024,512]{1,0:T(8,128)S(1)} %shard_map.109, bf16[1024,512]{1,0:T(8,128)(2,1)} %collective-permute-done.3), kind=kLoop, calls=%fused_computation.1 | loop fusion | flops 3670016 | bytes 8392704 | tf_op jit(solution)/shard_map/sub | solution.py:239
  159.0 5.7 %all-to-all-done.3.got = bf16[16,32,128]{2,1,0:T(8,128)(2,1)S(1)} async-done(((bf16[16,32,128]{2,1,0:T(8,128)(2,1)}), bf16[16,32,128]{2,1,0:T(8,128)(2,1)S(1)}, u32[]{:S(2)}, u32[]{:S(2)}) %all-to-all-start.3) | async-done | bytes 131104 | tf_op jit(solution)/shard_map/all_to_all | solution.py:175
  164.7 0.9 shard_map.110
  (34 shorter events, 1.7 us)
Async XLA Ops:
  0.6 1.0 copy-start
  1.7 37.0 %copy-start.10 = (f32[1024,512]{1,0:T(8,128)S(1)}, f32[1024,512]{1,0:T(8,128)}, u32[]{:S(2)}) copy-start(f32[1024,512]{1,0:T(8,128)} %param.7) | copy-start | bytes 6291460
  38.6 3.0 %copy-start.4 = (s32[2,4]{1,0:T(2,128)S(1)}, s32[2,4]{1,0:T(2,128)}, u32[]{:S(2)}) copy-start(s32[2,4]{1,0:T(2,128)} %relations.1) | copy-start | bytes 100
  38.6 3.0 %copy-start.7 = (s32[2,1024]{1,0:T(2,128)S(1)}, s32[2,1024]{1,0:T(2,128)}, u32[]{:S(2)}) copy-start(s32[2,1024]{1,0:T(2,128)} %head_at.3) | copy-start | bytes 24580
  38.6 5.4 %collective-permute-start = (bf16[4,512,256]{2,1,0:T(8,128)(2,1)S(1)}, bf16[4,512,256]{2,1,0:T(8,128)(2,1)S(1)}, u32[]{:S(2)}, u32[]{:S(2)}) collective-permute-start(bf16[4,512,256]{2,1,0:T(8,128)(2,1)S(1)} %bitcast.12), channel_id=1, source_target_pairs={{0,16},{16,0},{32,48},{48,32},{64,80},{80,64},{96,112},{112,96},{1... | collective-permute-start | bytes 3145736 | tf_op jit(solution)/shard_map/ppermute | solution.py:46
  38.8 25.6 %collective-permute-start.1 = (bf16[1024,512]{1,0:T(8,128)(2,1)S(1)}, bf16[1024,512]{1,0:T(8,128)(2,1)S(1)}, u32[]{:S(2)}, u32[]{:S(2)}) collective-permute-start(bf16[1024,512]{1,0:T(8,128)(2,1)S(1)} %convert_element_type.27.heads), channel_id=1, source_target_pairs={{0,1},{1,0},{2,3},{3,2},{4,5},{5,4},{6,7},{7,6},{8,9},{9,8},{10,11... | collective-permute-start | bytes 3145736 | tf_op jit(solution)/shard_map/ppermute | solution.py:46
  39.3 35.6 %collective-permute-start.2 = (bf16[1024,512]{1,0:T(8,128)(2,1)S(1)}, bf16[1024,512]{1,0:T(8,128)(2,1)S(1)}, u32[]{:S(2)}, u32[]{:S(2)}) collective-permute-start(bf16[1024,512]{1,0:T(8,128)(2,1)S(1)} %convert_element_type.27.heads), channel_id=1, source_target_pairs={{0,8},{1,9},{2,10},{3,11},{4,12},{5,13},{6,14},{7,15},{8,0},{9,1},... | collective-permute-start | bytes 3145736 | tf_op jit(solution)/shard_map/ppermute | solution.py:46
  41.6 2.4 %copy-start.11 = (s32[2,1024]{1,0:T(2,128)S(1)}, s32[2,1024]{1,0:T(2,128)}, u32[]{:S(2)}) copy-start(s32[2,1024]{1,0:T(2,128)} %param.12) | copy-start | bytes 24580
  44.1 1.3 copy-start.1
  72.0 1.0 copy-start.8
  83.9 1.0 copy-start.5
  84.9 4.5 %collective-permute-start.5 = (bf16[8,4,32,512]{3,2,1,0:T(8,128)(2,1)}, bf16[8,4,32,512]{3,2,1,0:T(8,128)(2,1)}, u32[]{:S(2)}, u32[]{:S(2)}) collective-permute-start(bf16[8,4,32,512]{3,2,1,0:T(8,128)(2,1)} %get-tuple-element.27), channel_id=1, source_target_pairs={{0,16},{16,0},{32,48},{48,32},{64,80},{80,64},{96,112},{112,96},{1... | collective-permute-start | bytes 3145736 | tf_op jit(solution)/shard_map/ppermute | solution.py:46
  84.9 34.8 %collective-permute-start.3 = (bf16[1024,512]{1,0:T(8,128)(2,1)}, bf16[1024,512]{1,0:T(8,128)(2,1)}, u32[]{:S(2)}, u32[]{:S(2)}) collective-permute-start(bf16[1024,512]{1,0:T(8,128)(2,1)} %get-tuple-element.24), channel_id=1, source_target_pairs={{0,1},{1,0},{2,3},{3,2},{4,5},{5,4},{6,7},{7,6},{8,9},{9,8},{10,11... | collective-permute-start | bytes 3145736 | tf_op jit(solution)/shard_map/ppermute | solution.py:46
  86.4 33.3 %collective-permute-start.4 = (bf16[1024,512]{1,0:T(8,128)(2,1)}, bf16[1024,512]{1,0:T(8,128)(2,1)}, u32[]{:S(2)}, u32[]{:S(2)}) collective-permute-start(bf16[1024,512]{1,0:T(8,128)(2,1)} %get-tuple-element.25), channel_id=1, source_target_pairs={{0,8},{1,9},{2,10},{3,11},{4,12},{5,13},{6,14},{7,15},{8,0},{9,1},... | collective-permute-start | bytes 3145736 | tf_op jit(solution)/shard_map/ppermute | solution.py:46
  92.0 32.3 %all-to-all-start.2 = ((bf16[8,4,32,512]{3,2,1,0:T(8,128)(2,1)}), bf16[8,4,32,512]{3,2,1,0:T(8,128)(2,1)}, u32[]{:S(2)}, u32[]{:S(2)}) async-start(bf16[8,4,32,512]{3,2,1,0:T(8,128)(2,1)} %add_convert_fusion), calls=%async_computation.2 | async-start | bytes 2097152 | tf_op jit(solution)/shard_map/all_to_all | solution.py:172
  99.6 1.2 copy-start.2
  100.8 1.2 copy-start.6
  102.1 1.2 copy-start.9
  107.6 14.1 %copy-start.12 = (f32[1024]{0:T(1024)S(1)}, f32[1024]{0:T(1024)}, u32[]{:S(2)}) copy-start(f32[1024]{0:T(1024)} %param.8) | copy-start | bytes 12292
  126.5 38.2 %all-to-all-start.3 = ((bf16[16,32,128]{2,1,0:T(8,128)(2,1)}), bf16[16,32,128]{2,1,0:T(8,128)(2,1)S(1)}, u32[]{:S(2)}, u32[]{:S(2)}) async-start(bf16[16,32,128]{2,1,0:T(8,128)(2,1)} %bitcast.7), calls=%async_computation.3 | async-start | bytes 262144 | tf_op jit(solution)/shard_map/all_to_all | solution.py:175
  154.9 9.8 %copy-start.3 = (f32[4,32,32]{2,1,0:T(8,128)S(1)}, f32[4,32,32]{2,1,0:T(8,128)}, u32[]{:S(2)}) copy-start(f32[4,32,32]{2,1,0:T(8,128)} %state.1) | copy-start | bytes 49156

commit v5 on v4

--- a/solution.py
+++ b/solution.py
@@ -13,6 +13,7 @@
 NT = (((1,), (1,)), ((), ()))
 TN = (((0,), (0,)), ((), ()))
 VMEM_BYTES = 24 << 20
+UPDATE_PARTS = 4
 
 
 def dot(a, b, dims):
@@ -131,7 +132,7 @@
         sent[:, r] = total[r, :, 1 - core[0]].astype(BF)
 
 
-def head_kernel(relations, core, head_at, grad0, grad1, own, other, total, part):
+def head_kernel(relations, core, head_at, grad0, grad1, own, other, near, total, part):
     batches = relations.shape[1]
     edges = grad0.shape[0] // batches
     parts = 4
@@ -147,9 +148,56 @@
             to = slice(k * step, (k + 1) * step)
             added = dot(picks(head_at[bucket : bucket + 1, :], k * step, step), part[...], NN)
             if bucket == 0:
-                total[to, :] = added
+                total[to, :] = added + near[to, :].astype(F32)
             else:
                 total[to, :] += added
+
+
+def update_kernel(far, head, table, state, new_table, new_state, held, into, out, out_done):
+    parts, block = into.shape[0], state.shape[1]
+    step = table.shape[0] // parts
+    spans = [pl.ds(part * step, step) for part in range(parts)]
+    coming = [pltpu.make_async_copy(far.at[to], held.at[to], into.at[part]) for part, to in enumerate(spans)]
+    leaving = [pltpu.make_async_copy(out.at[to], new_table.at[to], out_done.at[part]) for part, to in enumerate(spans)]
+    for copy in coming:
+        copy.start()
+    for part in range(parts):
+        coming[part].wait()
+        for first in range(part * step, (part + 1) * step, block):
+            at, row = slice(first, first + block), slice(first // block, first // block + 1)
+            grad = head[at, :] + held[at, :].astype(F32)
+            before = jnp.broadcast_to(state[row, :], (block, block)).T[:, :1]
+            sums = before + jnp.mean(grad * grad, axis=1, keepdims=True)
+            new_state[row, :] = jnp.broadcast_to(sums, (block, block)).T[:1, :]
+            out[at, :] = table[at, :] - grad * (LEARN_RATE / jnp.sqrt(sums))
+        leaving[part].start()
+    for copy in leaving:
+        copy.wait()
+
+
+def updated(head, far, table, state):
+    count, width = table.shape
+    block, parts = 128, UPDATE_PARTS
+    anywhere = pl.BlockSpec(memory_space=pl.ANY)
+    new_table, new_state = pl.pallas_call(
+        update_kernel,
+        out_shape=(
+            jax.ShapeDtypeStruct(table.shape, F32),
+            jax.ShapeDtypeStruct((count // block, block), F32),
+        ),
+        in_specs=[anywhere] + vmem(3),
+        out_specs=(anywhere, vmem(1)[0]),
+        scratch_shapes=[
+            pltpu.VMEM((count, width), BF),
+            pltpu.SemaphoreType.DMA((parts,)),
+            pltpu.VMEM((count, width), F32),
+            pltpu.SemaphoreType.DMA((parts,)),
+        ],
+        compiler_params=pltpu.CompilerParams(vmem_limit_bytes=VMEM_BYTES),
+        cost_estimate=pl.CostEstimate(flops=8 * table.size, bytes_accessed=16 * table.size, transcendentals=0),
+        name="update",
+    )(far, head, table, state.reshape(count // block, block))
+    return new_table, new_state.reshape(count)
 
 
 def op_update_kernel(got, state, operators, new_operators, new_state):
@@ -231,12 +279,10 @@
         3 * matmul,
         (((count, width), F32),),
         (batch_relation, core),
-        (head_index, *query_grads, half, other),
+        (head_index, *query_grads, half, other, returned[0]),
         (pltpu.VMEM((edges, width), BF),),
     )
-    entity_grad = head_total + returned[0].astype(F32) + returned[1].astype(F32)
-    new_state = row_state + jnp.mean(entity_grad * entity_grad, axis=1)
-    new_table = entity_table - LEARN_RATE * entity_grad / jnp.sqrt(new_state)[:, None]
+    new_table, new_state = updated(head_total, returned[1], entity_table, row_state)
     columns = width // wide_count
     first_column = lax.axis_index("wide") * columns
     own_operators = lax.dynamic_slice_in_dim(operators, first_column, columns, 2)

time: 168 us -> 162 us (0.964)
  starting transfers between devices: 43.2 us -> 34.6 us
  waiting for transfers between devices: 39.5 us -> 48 us
  other arithmetic: 10.9 us -> 3.03 us
  Pallas kernels: 26.7 us -> 29.2 us
    all_to_all x1, waiting for transfers between devices: 2.02 us -> 23.7 us  [summed_over_devices(): got = lax.all_to_all(pair, 'wide', 0, 0, axis_index_groups=groups)]
    ppermute x6, waiting for transfers between devices: 31.8 us -> 22 us  [swapped(): lax.ppermute(block, axis, [(i, i ^ 1 << stride) for i in range(count)])]
    all_to_all x1, starting transfers between devices: 28.4 us -> 19.4 us  [summed_over_devices(): return lax.all_to_all(part, 'narrow', 0, 0)]
    sub x1 -> x0, other arithmetic: 4.11 us -> none  [step(): entity_table - LEARN_RATE * entity_grad / jnp.sqrt(new_state)[:, None]]
    pallas_call x0 -> x1, Pallas kernels: none -> 3.86 us  [updated(): pl.pallas_call(update_kernel, out_shape=(jax.ShapeDtypeStruct(table.shape...]
    all_to_all x1, waiting for transfers between devices: 5.7 us -> 2.26 us  [summed_over_devices(): return lax.all_to_all(part, 'narrow', 0, 0)]
    reduce_sum x1 -> x0, other arithmetic: 2.06 us -> none  [step(): new_state = row_state + jnp.mean(entity_grad * entity_grad, axis=1)]
    unnamed x26 -> x30, local copies, waits for them, and re-layouts: 6.54 us -> 6.6 us
  transfers between devices with their start and end apart: 8 -> 8, of which waited for: 5 -> 5; matrix products, arithmetic and copies ran while one was open for 6% -> 3% of each run, Pallas kernels for 10% -> 13%
where the time goes in v5:
time: 162 us; the launch traced here: 161 us
  waiting for transfers between devices  48 us (30%)
  blocking collectives  36.8 us (23%)
  starting transfers between devices  34.6 us (21%)
  Pallas kernels  29.2 us (18%)
  local copies, waits for them, and re-layouts  8.29 us (5%)
  other arithmetic  3.03 us (2%)
    all_to_all x2, blocking collectives, spread(): return lax.all_to_all(sent, axis, 0, 0, axis_index_groups=groups)  36.8 us
    pallas_call x9, Pallas kernels, local(): pl.pallas_call(kernel, out_shape=shapes, in_specs=smem(len(scalars)) + vm...  25.4 us
    all_to_all x1, waiting for transfers between devices, summed_over_devices(): got = lax.all_to_all(pair, 'wide', 0, 0, axis_index_groups=groups)  23.7 us
    ppermute x6, waiting for transfers between devices, swapped(): lax.ppermute(block, axis, [(i, i ^ 1 << stride) for i in range(count)])  22 us
    all_to_all x1, starting transfers between devices, summed_over_devices(): return lax.all_to_all(part, 'narrow', 0, 0)  19.4 us
    ppermute x6, starting transfers between devices, swapped(): lax.ppermute(block, axis, [(i, i ^ 1 << stride) for i in range(count)])  7.7 us
    all_to_all x1, starting transfers between devices, summed_over_devices(): got = lax.all_to_all(pair, 'wide', 0, 0, axis_index_groups=groups)  7.49 us
    unnamed x30, local copies, waits for them, and re-layouts  6.6 us
  transfers between devices with their start and end apart: 8, of which 5 were waited for; matrix products, arithmetic and copies ran while one was open for 3% of the time, Pallas kernels for 13%

profile of v5, /device:TPU:4, one launch (start us, length us, event | category | flops | bytes accessed | tf_op | source)
XLA Modules:
  0.0 160.7 jit_solution(6243364642179318384)
XLA Ops:
  0.7 0.9 copy-done
  1.7 21.5 %all_to_all.20 = bf16[16,32,256]{2,1,0:T(8,128)(2,1)S(1)} all-to-all(bf16[16,32,256]{2,1,0:T(8,128)(2,1)S(1)} %broadcast_in_dim.7), channel_id=1, replica_groups=mesh['wide'=16,'narrow'=16] {'narrow'}, dimensions={0} | all-to-all | bytes 524288 | tf_op jit(solution)/shard_map/all_to_all | solution.py:56
  23.3 15.3 %all_to_all.21 = bf16[4,16,32,256]{3,2,1,0:T(8,128)(2,1)S(1)} all-to-all(bf16[4,16,32,256]{3,2,1,0:T(8,128)(2,1)S(1)} %broadcast_in_dim.16), channel_id=1, replica_groups={{0,64,128,192},{16,80,144,208},{32,96,160,224},{48,112,176,240},{1,65,1..., dimensions={0} | all-to-all | bytes 2097152 | tf_op jit(solution)/shard_map/all_to_all | solution.py:56
  39.3 2.3 %collective-permute-start.1 = (bf16[1024,512]{1,0:T(8,128)(2,1)S(1)}, bf16[1024,512]{1,0:T(8,128)(2,1)S(1)}, u32[]{:S(2)}, u32[]{:S(2)}) collective-permute-start(bf16[1024,512]{1,0:T(8,128)(2,1)S(1)} %convert_element_type.21.heads), channel_id=1, source_target_pairs={{0,8},{1,9},{2,10},{3,11},{4,12},{5,13},{6,14},{7,15},{8,0},{9,1},... | collective-permute-start | bytes 3145736 | tf_op jit(solution)/shard_map/ppermute | solution.py:47
  41.6 2.4 %shard_map.102 = (bf16[1024,512]{1,0:T(8,128)(2,1)S(1)}, bf16[1024,512]{1,0:T(8,128)(2,1)S(1)}) custom-call(s32[2,1024]{1,0:T(2,128)S(1)} %copy-done.11, bf16[1024,512]{1,0:T(8,128)(2,1)S(1)} %convert_element_type.21.heads), custom_call_target="tpu_custom_call" | custom-call | flops 2147483648 | bytes 3153920 | tf_op jit(solution)/shard_map/pallas_call | solution.py:34
  44.1 1.3 shard_map.105.query
  45.4 1.3 shard_map.103.query
  46.7 17.8 %collective-permute-done.3.tails = bf16[1024,512]{1,0:T(8,128)(2,1)S(1)} collective-permute-done((bf16[1024,512]{1,0:T(8,128)(2,1)S(1)}, bf16[1024,512]{1,0:T(8,128)(2,1)S(1)}, u32[]{:S(2)}, u32[]{:S(2)}) %collective-permute-start.3) | collective-permute-done | bytes 1048608 | tf_op jit(solution)/shard_map/ppermute | solution.py:47
  64.4 4.8 %shard_map.106 = (bf16[1024,1024]{1,0:T(8,128)(2,1)S(1)}, bf16[1024,512]{1,0:T(8,128)(2,1)}) custom-call(bf16[1024,512]{1,0:T(8,128)(2,1)S(1)} %shard_map.105.query, bf16[1024,512]{1,0:T(8,128)(2,1)S(1)} %collective-permute-done.3.tails, s32[1,1024]{1,0:T(1,128)S(1)} %get-tuple-element.34.tail_at), custom_call_target="tpu_custom_call" | custom-call | flops 4294967296 | bytes 5246976 | tf_op jit(solution)/shard_map/pallas_call | solution.py:34
  69.2 2.7 %shard_map.107 = (bf16[1024,512]{1,0:T(8,128)(2,1)S(1)}, f32[4,8,2,32,512]{4,3,2,1,0:T(8,128)S(1)}) custom-call(s32[4]{0:T(128)S(1)} %get-tuple-element.36.relations, bf16[1024,1024]{1,0:T(8,128)(2,1)S(1)} %get-tuple-element.22.score_grad, bf16[1024,512]{1,0:T(8,128)(2,1)S(1)} %collective-permute-done.3.tails, bf16[1024,512]{1,0:T(8,128)(2,1)S(1)} %get-tuple-element.21.rows), custom_call_target="tpu_custom_call" | custom-call | flops 2147483648 | bytes 9437184 | tf_op jit(solution)/shard_map/pallas_call | solution.py:34
  71.9 3.0 %collective-permute-done.1.tails = bf16[1024,512]{1,0:T(8,128)(2,1)S(1)} collective-permute-done((bf16[1024,512]{1,0:T(8,128)(2,1)S(1)}, bf16[1024,512]{1,0:T(8,128)(2,1)S(1)}, u32[]{:S(2)}, u32[]{:S(2)}) %collective-permute-start.1) | collective-permute-done | bytes 1048608 | tf_op jit(solution)/shard_map/ppermute | solution.py:47
  75.0 3.8 %shard_map.104 = (bf16[1024,1024]{1,0:T(8,128)(2,1)S(1)}, bf16[1024,512]{1,0:T(8,128)(2,1)S(1)}) custom-call(bf16[1024,512]{1,0:T(8,128)(2,1)S(1)} %shard_map.103.query, bf16[1024,512]{1,0:T(8,128)(2,1)S(1)} %collective-permute-done.1.tails, s32[1,1024]{1,0:T(1,128)S(1)} %get-tuple-element.35.tail_at), custom_call_target="tpu_custom_call" | custom-call | flops 4294967296 | bytes 5246976 | tf_op jit(solution)/shard_map/pallas_call | solution.py:34
  78.8 1.0 copy-done.8
  79.8 3.2 %shard_map.108 = (bf16[1024,512]{1,0:T(8,128)(2,1)S(1)}, f32[8,4,32,512]{3,2,1,0:T(8,128)S(1)}, bf16[8,4,32,512]{3,2,1,0:T(8,128)(2,1)S(1)}) custom-call(s32[4]{0:T(128)S(1)} %get-tuple-element.37.relations, s32[1]{0:T(128)} %bitcast.1.core, bf16[1024,1024]{1,0:T(8,128)(2,1)S(1)} %get-tuple-element.24.score_grad, ...), custom_call_target="tpu_custom_call" | custom-call | flops 2147483648 | bytes 12582912 | tf_op jit(solution)/shard_map/pallas_call | solution.py:34
  82.9 1.0 copy-done.9
  84.0 1.5 collective-permute-start.4
  85.4 1.2 collective-permute-done.5
  86.6 1.5 add_convert_fusion
  88.1 7.5 %all-to-all-start.2 = ((bf16[8,4,32,512]{3,2,1,0:T(8,128)(2,1)}), bf16[8,4,32,512]{3,2,1,0:T(8,128)(2,1)}, u32[]{:S(2)}, u32[]{:S(2)}) async-start(bf16[8,4,32,512]{3,2,1,0:T(8,128)(2,1)} %add_convert_fusion), calls=%async_computation.2 | async-start | bytes 2097152 | tf_op jit(solution)/shard_map/all_to_all | solution.py:220
  95.6 3.4 %collective-permute-start.2 = (bf16[1024,512]{1,0:T(8,128)(2,1)}, bf16[1024,512]{1,0:T(8,128)(2,1)}, u32[]{:S(2)}, u32[]{:S(2)}) collective-permute-start(bf16[1024,512]{1,0:T(8,128)(2,1)} %copy-done.8), channel_id=1, source_target_pairs={{0,8},{1,9},{2,10},{3,11},{4,12},{5,13},{6,14},{7,15},{8,0},{9,1},... | collective-permute-start | bytes 3145736 | tf_op jit(solution)/shard_map/ppermute | solution.py:47
  99.0 0.7 constant_dynamic-slice_fusion.operators
  99.7 23.7 %all-to-all-done.2 = bf16[8,4,32,512]{3,2,1,0:T(8,128)(2,1)} async-done(((bf16[8,4,32,512]{3,2,1,0:T(8,128)(2,1)}), bf16[8,4,32,512]{3,2,1,0:T(8,128)(2,1)}, u32[]{:S(2)}, u32[]{:S(2)}) %all-to-all-start.2) | async-done | bytes 1048608 | tf_op jit(solution)/shard_map/all_to_all | solution.py:220
  123.4 1.4 reduce_sum.12
  124.8 0.7 copy.11
  125.6 19.4 %all-to-all-start.3 = ((bf16[16,32,128]{2,1,0:T(8,128)(2,1)}), bf16[16,32,128]{2,1,0:T(8,128)(2,1)S(1)}, u32[]{:S(2)}, u32[]{:S(2)}) async-start(bf16[16,32,128]{2,1,0:T(8,128)(2,1)} %bitcast.20), calls=%async_computation.3 | async-start | bytes 262144 | tf_op jit(solution)/shard_map/all_to_all | solution.py:223
  144.9 1.2 copy-done.3
  146.2 1.2 copy-done.10
  147.4 1.2 copy-done.13
  148.6 5.0 %shard_map.109.head = f32[1024,512]{1,0:T(8,128)S(1)} custom-call(s32[2,4]{1,0:T(2,128)S(1)} %copy-done.7, s32[1]{0:T(128)} %bitcast.1.core, s32[2,1024]{1,0:T(2,128)S(1)} %copy-done.11, bf16[1024,512]{1,0:T(8,128)(2,1)S(1)} %copy-done.13, bf16[1024,512]{1,0:T(8,128)(2,1)S(1)} %copy-done.10, bf16[4,512,256]{2,1,0:T(8,128)(2,1)S(1)} %bitcast.17, ...), custom_call_target="tpu_custom_call" | custom-call | flops 3221225472 | bytes 7348224 | tf_op jit(solution)/shard_map/pallas_call | solution.py:34
  153.7 3.9 %update.1 = (f32[1024,512]{1,0:T(8,128)}, f32[8,128]{1,0:T(8,128)}) custom-call(bf16[1024,512]{1,0:T(8,128)(2,1)} %collective-permute-done.2.far, f32[1024,512]{1,0:T(8,128)S(1)} %shard_map.109.head, f32[1024,512]{1,0:T(8,128)S(1)} %copy-done.1, f32[8,128]{1,0:T(8,128)S(1)} %bitcast.18), custom_call_target="tpu_custom_call" | custom-call | flops 4194304 | bytes 8388608 | tf_op jit(solution)/shard_map/update/pallas_call | solution.py:182
  157.6 2.3 %all-to-all-done.3.got = bf16[16,32,128]{2,1,0:T(8,128)(2,1)S(1)} async-done(((bf16[16,32,128]{2,1,0:T(8,128)(2,1)}), bf16[16,32,128]{2,1,0:T(8,128)(2,1)S(1)}, u32[]{:S(2)}, u32[]{:S(2)}) %all-to-all-start.3) | async-done | bytes 131104 | tf_op jit(solution)/shard_map/all_to_all | solution.py:223
  159.9 0.9 shard_map.110
  (36 shorter events, 1.0 us)
Async XLA Ops:
  0.6 1.0 copy-start
  1.7 37.0 %copy-start.1 = (f32[1024,512]{1,0:T(8,128)S(1)}, f32[1024,512]{1,0:T(8,128)}, u32[]{:S(2)}) copy-start(f32[1024,512]{1,0:T(8,128)} %table.1) | copy-start | bytes 6291460
  38.6 3.0 %copy-start.7 = (s32[2,4]{1,0:T(2,128)S(1)}, s32[2,4]{1,0:T(2,128)}, u32[]{:S(2)}) copy-start(s32[2,4]{1,0:T(2,128)} %relations.1) | copy-start | bytes 100
  38.6 3.0 %copy-start.11 = (s32[2,1024]{1,0:T(2,128)S(1)}, s32[2,1024]{1,0:T(2,128)}, u32[]{:S(2)}) copy-start(s32[2,1024]{1,0:T(2,128)} %head_at.3) | copy-start | bytes 24580
  38.6 5.4 %collective-permute-start = (bf16[4,512,256]{2,1,0:T(8,128)(2,1)S(1)}, bf16[4,512,256]{2,1,0:T(8,128)(2,1)S(1)}, u32[]{:S(2)}, u32[]{:S(2)}) collective-permute-start(bf16[4,512,256]{2,1,0:T(8,128)(2,1)S(1)} %bitcast.14), channel_id=1, source_target_pairs={{0,16},{16,0},{32,48},{48,32},{64,80},{80,64},{96,112},{112,96},{1... | collective-permute-start | bytes 3145736 | tf_op jit(solution)/shard_map/ppermute | solution.py:47
  38.8 25.6 %collective-permute-start.3 = (bf16[1024,512]{1,0:T(8,128)(2,1)S(1)}, bf16[1024,512]{1,0:T(8,128)(2,1)S(1)}, u32[]{:S(2)}, u32[]{:S(2)}) collective-permute-start(bf16[1024,512]{1,0:T(8,128)(2,1)S(1)} %convert_element_type.21.heads), channel_id=1, source_target_pairs={{0,1},{1,0},{2,3},{3,2},{4,5},{5,4},{6,7},{7,6},{8,9},{9,8},{10,11... | collective-permute-start | bytes 3145736 | tf_op jit(solution)/shard_map/ppermute | solution.py:47
  39.3 35.6 %collective-permute-start.1 = (bf16[1024,512]{1,0:T(8,128)(2,1)S(1)}, bf16[1024,512]{1,0:T(8,128)(2,1)S(1)}, u32[]{:S(2)}, u32[]{:S(2)}) collective-permute-start(bf16[1024,512]{1,0:T(8,128)(2,1)S(1)} %convert_element_type.21.heads), channel_id=1, source_target_pairs={{0,8},{1,9},{2,10},{3,11},{4,12},{5,13},{6,14},{7,15},{8,0},{9,1},... | collective-permute-start | bytes 3145736 | tf_op jit(solution)/shard_map/ppermute | solution.py:47
  41.6 2.4 %copy-start.14 = (s32[2,1024]{1,0:T(2,128)S(1)}, s32[2,1024]{1,0:T(2,128)}, u32[]{:S(2)}) copy-start(s32[2,1024]{1,0:T(2,128)} %param.12) | copy-start | bytes 24580
  44.1 1.3 copy-start.2
  71.9 6.8 %copy-start.12 = (bf16[1024,512]{1,0:T(8,128)(2,1)}, bf16[1024,512]{1,0:T(8,128)(2,1)S(1)}, u32[]{:S(2)}) copy-start(bf16[1024,512]{1,0:T(8,128)(2,1)S(1)} %get-tuple-element.23.grad0) | copy-start | bytes 3145732
  78.8 1.0 copy-start.8
  82.9 1.0 copy-start.9
  84.0 2.7 %collective-permute-start.5 = (bf16[8,4,32,512]{3,2,1,0:T(8,128)(2,1)S(1)}, bf16[8,4,32,512]{3,2,1,0:T(8,128)(2,1)S(1)}, u32[]{:S(2)}, u32[]{:S(2)}) collective-permute-start(bf16[8,4,32,512]{3,2,1,0:T(8,128)(2,1)S(1)} %get-tuple-element.31), channel_id=1, source_target_pairs={{0,16},{16,0},{32,48},{48,32},{64,80},{80,64},{96,112},{112,96},{1... | collective-permute-start | bytes 3145736 | tf_op jit(solution)/shard_map/ppermute | solution.py:47
  84.0 61.0 %collective-permute-start.4 = (bf16[1024,512]{1,0:T(8,128)(2,1)}, bf16[1024,512]{1,0:T(8,128)(2,1)}, u32[]{:S(2)}, u32[]{:S(2)}) collective-permute-start(bf16[1024,512]{1,0:T(8,128)(2,1)} %get-tuple-element.27), channel_id=1, source_target_pairs={{0,1},{1,0},{2,3},{3,2},{4,5},{5,4},{6,7},{7,6},{8,9},{9,8},{10,11... | collective-permute-start | bytes 3145736 | tf_op jit(solution)/shard_map/ppermute | solution.py:47
  88.1 35.3 %all-to-all-start.2 = ((bf16[8,4,32,512]{3,2,1,0:T(8,128)(2,1)}), bf16[8,4,32,512]{3,2,1,0:T(8,128)(2,1)}, u32[]{:S(2)}, u32[]{:S(2)}) async-start(bf16[8,4,32,512]{3,2,1,0:T(8,128)(2,1)} %add_convert_fusion), calls=%async_computation.2 | async-start | bytes 2097152 | tf_op jit(solution)/shard_map/all_to_all | solution.py:220
  95.6 58.1 %collective-permute-start.2 = (bf16[1024,512]{1,0:T(8,128)(2,1)}, bf16[1024,512]{1,0:T(8,128)(2,1)}, u32[]{:S(2)}, u32[]{:S(2)}) collective-permute-start(bf16[1024,512]{1,0:T(8,128)(2,1)} %copy-done.8), channel_id=1, source_target_pairs={{0,8},{1,9},{2,10},{3,11},{4,12},{5,13},{6,14},{7,15},{8,0},{9,1},... | collective-permute-start | bytes 3145736 | tf_op jit(solution)/shard_map/ppermute | solution.py:47
  125.6 34.3 %all-to-all-start.3 = ((bf16[16,32,128]{2,1,0:T(8,128)(2,1)}), bf16[16,32,128]{2,1,0:T(8,128)(2,1)S(1)}, u32[]{:S(2)}, u32[]{:S(2)}) async-start(bf16[16,32,128]{2,1,0:T(8,128)(2,1)} %bitcast.20), calls=%async_computation.3 | async-start | bytes 262144 | tf_op jit(solution)/shard_map/all_to_all | solution.py:223
  144.9 1.2 copy-start.3
  146.2 1.2 copy-start.10
  147.4 1.2 copy-start.13
  148.6 5.1 %copy-start.6 = (f32[1024]{0:T(1024)S(1)}, f32[1024]{0:T(1024)}, u32[]{:S(2)}) copy-start(f32[1024]{0:T(1024)} %param.8) | copy-start | bytes 12292
  153.7 6.2 %copy-start.4 = (f32[4,32,32]{2,1,0:T(8,128)S(1)}, f32[4,32,32]{2,1,0:T(8,128)}, u32[]{:S(2)}) copy-start(f32[4,32,32]{2,1,0:T(8,128)} %constant_dynamic-slice_fusion.operators) | copy-start | bytes 49156
  153.7 6.1 %copy-start.5 = (f32[4,32,32]{2,1,0:T(8,128)S(1)}, f32[4,32,32]{2,1,0:T(8,128)}, u32[]{:S(2)}) copy-start(f32[4,32,32]{2,1,0:T(8,128)} %state.1) | copy-start | bytes 49156

commit v6 on v5

--- a/solution.py
+++ b/solution.py
@@ -13,7 +13,7 @@
 NT = (((1,), (1,)), ((), ()))
 TN = (((0,), (0,)), ((), ()))
 VMEM_BYTES = 24 << 20
-UPDATE_PARTS = 4
+UPDATE_PARTS = 8
 
 
 def dot(a, b, dims):
@@ -98,14 +98,16 @@
 
 def score_kernel(query, tails, tail_at, score_grad, tail_grad):
     count, edges = tails.shape[0], query.shape[0]
-    parts = 4
-    step = edges // parts
-    for part in range(parts):
+    step, block = edges // 4, count // 4
+    for part in range(4):
         at = slice(part * step, (part + 1) * step)
-        weights = jnp.exp(dot(tails[...], query[at, :], NT))
-        weights = weights * (1.0 / jnp.sum(weights, axis=0, keepdims=True))
-        hit = tail_at[:, at] == lax.broadcasted_iota(jnp.int32, (count, step), 0)
-        score_grad[:, at] = jnp.where(hit, weights - 1.0, weights).astype(BF)
+        weights = [jnp.exp(dot(tails[k * block : (k + 1) * block, :], query[at, :], NT)) for k in range(4)]
+        scale = 1.0 / sum(jnp.sum(w, axis=0, keepdims=True) for w in weights)
+        spot = lax.broadcasted_iota(jnp.int32, (block, step), 0)
+        for k, w in enumerate(weights):
+            share = w * scale
+            hit = tail_at[:, at] - k * block == spot
+            score_grad[k * block : (k + 1) * block, at] = jnp.where(hit, share - 1.0, share).astype(BF)
     tail_grad[...] = dot(score_grad[...], query[...], NN).astype(BF)
 
 
@@ -242,11 +244,7 @@
     score_grads, returned, query_grads = [None, None], [None, None], [None, None]
     for bucket in (0, 1):
         (query,) = local(
-            query_kernel,
-            matmul // 2,
-            (flat,),
-            (batch_relation[bucket], core),
-            (rows[bucket], half, other),
+            query_kernel, matmul // 2, (flat,), (batch_relation[bucket], core), (rows[bucket], half, other)
         )
         score_grads[bucket], tail_grad = local(
             score_kernel,

time: 162 us -> 162 us (level)
  no operation moved by 1% of the time
where the time goes in v6:
time: 162 us; the launch traced here: 160 us
  waiting for transfers between devices  47.7 us (29%)
  blocking collectives  36.8 us (23%)
  starting transfers between devices  34.5 us (21%)
  Pallas kernels  29.3 us (18%)
  local copies, waits for them, and re-layouts  8.29 us (5%)
  other arithmetic  3.03 us (2%)
    all_to_all x2, blocking collectives, spread(): return lax.all_to_all(sent, axis, 0, 0, axis_index_groups=groups)  36.8 us
    pallas_call x9, Pallas kernels, local(): pl.pallas_call(kernel, out_shape=shapes, in_specs=smem(len(scalars)) + vm...  24.9 us
    all_to_all x1, waiting for transfers between devices, summed_over_devices(): got = lax.all_to_all(pair, 'wide', 0, 0, axis_index_groups=groups)  23.7 us
    ppermute x6, waiting for transfers between devices, swapped(): lax.ppermute(block, axis, [(i, i ^ 1 << stride) for i in range(count)])  22.2 us
    all_to_all x1, starting transfers between devices, summed_over_devices(): return lax.all_to_all(part, 'narrow', 0, 0)  19.4 us
    ppermute x6, starting transfers between devices, swapped(): lax.ppermute(block, axis, [(i, i ^ 1 << stride) for i in range(count)])  7.67 us
    all_to_all x1, starting transfers between devices, summed_over_devices(): got = lax.all_to_all(pair, 'wide', 0, 0, axis_index_groups=groups)  7.49 us
    unnamed x30, local copies, waits for them, and re-layouts  6.6 us
  transfers between devices with their start and end apart: 8, of which 5 were waited for; matrix products, arithmetic and copies ran while one was open for 3% of the time, Pallas kernels for 13%

profile of v6, /device:TPU:4, one launch (start us, length us, event | category | flops | bytes accessed | tf_op | source)
XLA Modules:
  0.0 160.5 jit_solution(588607968873412018)
XLA Ops:
  0.7 0.9 copy-done
  1.7 21.5 %all_to_all.20 = bf16[16,32,256]{2,1,0:T(8,128)(2,1)S(1)} all-to-all(bf16[16,32,256]{2,1,0:T(8,128)(2,1)S(1)} %broadcast_in_dim.7), channel_id=1, replica_groups=mesh['wide'=16,'narrow'=16] {'narrow'}, dimensions={0} | all-to-all | bytes 524288 | tf_op jit(solution)/shard_map/all_to_all | solution.py:56
  23.3 15.3 %all_to_all.21 = bf16[4,16,32,256]{3,2,1,0:T(8,128)(2,1)S(1)} all-to-all(bf16[4,16,32,256]{3,2,1,0:T(8,128)(2,1)S(1)} %broadcast_in_dim.16), channel_id=1, replica_groups={{0,64,128,192},{16,80,144,208},{32,96,160,224},{48,112,176,240},{1,65,1..., dimensions={0} | all-to-all | bytes 2097152 | tf_op jit(solution)/shard_map/all_to_all | solution.py:56
  39.3 2.3 %collective-permute-start.1 = (bf16[1024,512]{1,0:T(8,128)(2,1)S(1)}, bf16[1024,512]{1,0:T(8,128)(2,1)S(1)}, u32[]{:S(2)}, u32[]{:S(2)}) collective-permute-start(bf16[1024,512]{1,0:T(8,128)(2,1)S(1)} %convert_element_type.21.heads), channel_id=1, source_target_pairs={{0,8},{1,9},{2,10},{3,11},{4,12},{5,13},{6,14},{7,15},{8,0},{9,1},... | collective-permute-start | bytes 3145736 | tf_op jit(solution)/shard_map/ppermute | solution.py:47
  41.6 2.4 %shard_map.102 = (bf16[1024,512]{1,0:T(8,128)(2,1)S(1)}, bf16[1024,512]{1,0:T(8,128)(2,1)S(1)}) custom-call(s32[2,1024]{1,0:T(2,128)S(1)} %copy-done.11, bf16[1024,512]{1,0:T(8,128)(2,1)S(1)} %convert_element_type.21.heads), custom_call_target="tpu_custom_call" | custom-call | flops 2147483648 | bytes 3153920 | tf_op jit(solution)/shard_map/pallas_call | solution.py:34
  44.1 1.3 shard_map.105.query
  45.4 1.3 shard_map.103.query
  46.7 17.8 %collective-permute-done.3.tails = bf16[1024,512]{1,0:T(8,128)(2,1)S(1)} collective-permute-done((bf16[1024,512]{1,0:T(8,128)(2,1)S(1)}, bf16[1024,512]{1,0:T(8,128)(2,1)S(1)}, u32[]{:S(2)}, u32[]{:S(2)}) %collective-permute-start.3) | collective-permute-done | bytes 1048608 | tf_op jit(solution)/shard_map/ppermute | solution.py:47
  64.4 4.6 %shard_map.106 = (bf16[1024,1024]{1,0:T(8,128)(2,1)S(1)}, bf16[1024,512]{1,0:T(8,128)(2,1)}) custom-call(bf16[1024,512]{1,0:T(8,128)(2,1)S(1)} %shard_map.105.query, bf16[1024,512]{1,0:T(8,128)(2,1)S(1)} %collective-permute-done.3.tails, s32[1,1024]{1,0:T(1,128)S(1)} %get-tuple-element.34.tail_at), custom_call_target="tpu_custom_call" | custom-call | flops 4294967296 | bytes 5246976 | tf_op jit(solution)/shard_map/pallas_call | solution.py:34
  69.0 2.7 %shard_map.107 = (bf16[1024,512]{1,0:T(8,128)(2,1)S(1)}, f32[4,8,2,32,512]{4,3,2,1,0:T(8,128)S(1)}) custom-call(s32[4]{0:T(128)S(1)} %get-tuple-element.36.relations, bf16[1024,1024]{1,0:T(8,128)(2,1)S(1)} %get-tuple-element.22.score_grad, bf16[1024,512]{1,0:T(8,128)(2,1)S(1)} %collective-permute-done.3.tails, bf16[1024,512]{1,0:T(8,128)(2,1)S(1)} %get-tuple-element.21.rows), custom_call_target="tpu_custom_call" | custom-call | flops 2147483648 | bytes 9437184 | tf_op jit(solution)/shard_map/pallas_call | solution.py:34
  71.7 3.2 %collective-permute-done.1.tails = bf16[1024,512]{1,0:T(8,128)(2,1)S(1)} collective-permute-done((bf16[1024,512]{1,0:T(8,128)(2,1)S(1)}, bf16[1024,512]{1,0:T(8,128)(2,1)S(1)}, u32[]{:S(2)}, u32[]{:S(2)}) %collective-permute-start.1) | collective-permute-done | bytes 1048608 | tf_op jit(solution)/shard_map/ppermute | solution.py:47
  75.0 3.6 %shard_map.104 = (bf16[1024,1024]{1,0:T(8,128)(2,1)S(1)}, bf16[1024,512]{1,0:T(8,128)(2,1)S(1)}) custom-call(bf16[1024,512]{1,0:T(8,128)(2,1)S(1)} %shard_map.103.query, bf16[1024,512]{1,0:T(8,128)(2,1)S(1)} %collective-permute-done.1.tails, s32[1,1024]{1,0:T(1,128)S(1)} %get-tuple-element.35.tail_at), custom_call_target="tpu_custom_call" | custom-call | flops 4294967296 | bytes 5246976 | tf_op jit(solution)/shard_map/pallas_call | solution.py:34
  78.6 1.0 copy-done.8
  79.5 3.2 %shard_map.108 = (bf16[1024,512]{1,0:T(8,128)(2,1)S(1)}, f32[8,4,32,512]{3,2,1,0:T(8,128)S(1)}, bf16[8,4,32,512]{3,2,1,0:T(8,128)(2,1)S(1)}) custom-call(s32[4]{0:T(128)S(1)} %get-tuple-element.37.relations, s32[1]{0:T(128)} %bitcast.1.core, bf16[1024,1024]{1,0:T(8,128)(2,1)S(1)} %get-tuple-element.24.score_grad, ...), custom_call_target="tpu_custom_call" | custom-call | flops 2147483648 | bytes 12582912 | tf_op jit(solution)/shard_map/pallas_call | solution.py:34
  82.7 1.0 copy-done.9
  83.7 1.4 collective-permute-start.4
  85.1 1.2 collective-permute-done.5
  86.4 1.5 add_convert_fusion
  87.9 7.5 %all-to-all-start.2 = ((bf16[8,4,32,512]{3,2,1,0:T(8,128)(2,1)}), bf16[8,4,32,512]{3,2,1,0:T(8,128)(2,1)}, u32[]{:S(2)}, u32[]{:S(2)}) async-start(bf16[8,4,32,512]{3,2,1,0:T(8,128)(2,1)} %add_convert_fusion), calls=%async_computation.2 | async-start | bytes 2097152 | tf_op jit(solution)/shard_map/all_to_all | solution.py:222
  95.4 3.4 %collective-permute-start.2 = (bf16[1024,512]{1,0:T(8,128)(2,1)}, bf16[1024,512]{1,0:T(8,128)(2,1)}, u32[]{:S(2)}, u32[]{:S(2)}) collective-permute-start(bf16[1024,512]{1,0:T(8,128)(2,1)} %copy-done.8), channel_id=1, source_target_pairs={{0,8},{1,9},{2,10},{3,11},{4,12},{5,13},{6,14},{7,15},{8,0},{9,1},... | collective-permute-start | bytes 3145736 | tf_op jit(solution)/shard_map/ppermute | solution.py:47
  98.7 0.7 constant_dynamic-slice_fusion.operators
  99.5 23.7 %all-to-all-done.2 = bf16[8,4,32,512]{3,2,1,0:T(8,128)(2,1)} async-done(((bf16[8,4,32,512]{3,2,1,0:T(8,128)(2,1)}), bf16[8,4,32,512]{3,2,1,0:T(8,128)(2,1)}, u32[]{:S(2)}, u32[]{:S(2)}) %all-to-all-start.2) | async-done | bytes 1048608 | tf_op jit(solution)/shard_map/all_to_all | solution.py:222
  123.2 1.4 reduce_sum.12
  124.5 0.7 copy.11
  125.3 19.4 %all-to-all-start.3 = ((bf16[16,32,128]{2,1,0:T(8,128)(2,1)}), bf16[16,32,128]{2,1,0:T(8,128)(2,1)S(1)}, u32[]{:S(2)}, u32[]{:S(2)}) async-start(bf16[16,32,128]{2,1,0:T(8,128)(2,1)} %bitcast.20), calls=%async_computation.3 | async-start | bytes 262144 | tf_op jit(solution)/shard_map/all_to_all | solution.py:225
  144.7 1.2 copy-done.3
  145.9 1.2 copy-done.10
  147.1 1.2 copy-done.13
  148.4 5.0 %shard_map.109.head = f32[1024,512]{1,0:T(8,128)S(1)} custom-call(s32[2,4]{1,0:T(2,128)S(1)} %copy-done.7, s32[1]{0:T(128)} %bitcast.1.core, s32[2,1024]{1,0:T(2,128)S(1)} %copy-done.11, bf16[1024,512]{1,0:T(8,128)(2,1)S(1)} %copy-done.13, bf16[1024,512]{1,0:T(8,128)(2,1)S(1)} %copy-done.10, bf16[4,512,256]{2,1,0:T(8,128)(2,1)S(1)} %bitcast.17, ...), custom_call_target="tpu_custom_call" | custom-call | flops 3221225472 | bytes 7348224 | tf_op jit(solution)/shard_map/pallas_call | solution.py:34
  153.5 4.4 %update.1 = (f32[1024,512]{1,0:T(8,128)}, f32[8,128]{1,0:T(8,128)}) custom-call(bf16[1024,512]{1,0:T(8,128)(2,1)} %collective-permute-done.2.far, f32[1024,512]{1,0:T(8,128)S(1)} %shard_map.109.head, f32[1024,512]{1,0:T(8,128)S(1)} %copy-done.1, f32[8,128]{1,0:T(8,128)S(1)} %bitcast.18), custom_call_target="tpu_custom_call" | custom-call | flops 4194304 | bytes 8388608 | tf_op jit(solution)/shard_map/update/pallas_call | solution.py:184
  157.8 1.8 %all-to-all-done.3.got = bf16[16,32,128]{2,1,0:T(8,128)(2,1)S(1)} async-done(((bf16[16,32,128]{2,1,0:T(8,128)(2,1)}), bf16[16,32,128]{2,1,0:T(8,128)(2,1)S(1)}, u32[]{:S(2)}, u32[]{:S(2)}) %all-to-all-start.3) | async-done | bytes 131104 | tf_op jit(solution)/shard_map/all_to_all | solution.py:225
  159.6 0.9 shard_map.110
  (36 shorter events, 1.0 us)
Async XLA Ops:
  0.6 1.0 copy-start
  1.7 37.0 %copy-start.1 = (f32[1024,512]{1,0:T(8,128)S(1)}, f32[1024,512]{1,0:T(8,128)}, u32[]{:S(2)}) copy-start(f32[1024,512]{1,0:T(8,128)} %table.1) | copy-start | bytes 6291460
  38.6 3.0 %copy-start.7 = (s32[2,4]{1,0:T(2,128)S(1)}, s32[2,4]{1,0:T(2,128)}, u32[]{:S(2)}) copy-start(s32[2,4]{1,0:T(2,128)} %relations.1) | copy-start | bytes 100
  38.6 3.0 %copy-start.11 = (s32[2,1024]{1,0:T(2,128)S(1)}, s32[2,1024]{1,0:T(2,128)}, u32[]{:S(2)}) copy-start(s32[2,1024]{1,0:T(2,128)} %head_at.3) | copy-start | bytes 24580
  38.6 5.4 %collective-permute-start = (bf16[4,512,256]{2,1,0:T(8,128)(2,1)S(1)}, bf16[4,512,256]{2,1,0:T(8,128)(2,1)S(1)}, u32[]{:S(2)}, u32[]{:S(2)}) collective-permute-start(bf16[4,512,256]{2,1,0:T(8,128)(2,1)S(1)} %bitcast.14), channel_id=1, source_target_pairs={{0,16},{16,0},{32,48},{48,32},{64,80},{80,64},{96,112},{112,96},{1... | collective-permute-start | bytes 3145736 | tf_op jit(solution)/shard_map/ppermute | solution.py:47
  38.8 25.6 %collective-permute-start.3 = (bf16[1024,512]{1,0:T(8,128)(2,1)S(1)}, bf16[1024,512]{1,0:T(8,128)(2,1)S(1)}, u32[]{:S(2)}, u32[]{:S(2)}) collective-permute-start(bf16[1024,512]{1,0:T(8,128)(2,1)S(1)} %convert_element_type.21.heads), channel_id=1, source_target_pairs={{0,1},{1,0},{2,3},{3,2},{4,5},{5,4},{6,7},{7,6},{8,9},{9,8},{10,11... | collective-permute-start | bytes 3145736 | tf_op jit(solution)/shard_map/ppermute | solution.py:47
  39.3 35.6 %collective-permute-start.1 = (bf16[1024,512]{1,0:T(8,128)(2,1)S(1)}, bf16[1024,512]{1,0:T(8,128)(2,1)S(1)}, u32[]{:S(2)}, u32[]{:S(2)}) collective-permute-start(bf16[1024,512]{1,0:T(8,128)(2,1)S(1)} %convert_element_type.21.heads), channel_id=1, source_target_pairs={{0,8},{1,9},{2,10},{3,11},{4,12},{5,13},{6,14},{7,15},{8,0},{9,1},... | collective-permute-start | bytes 3145736 | tf_op jit(solution)/shard_map/ppermute | solution.py:47
  41.6 2.4 %copy-start.14 = (s32[2,1024]{1,0:T(2,128)S(1)}, s32[2,1024]{1,0:T(2,128)}, u32[]{:S(2)}) copy-start(s32[2,1024]{1,0:T(2,128)} %param.12) | copy-start | bytes 24580
  44.1 1.3 copy-start.2
  71.7 6.8 %copy-start.12 = (bf16[1024,512]{1,0:T(8,128)(2,1)}, bf16[1024,512]{1,0:T(8,128)(2,1)S(1)}, u32[]{:S(2)}) copy-start(bf16[1024,512]{1,0:T(8,128)(2,1)S(1)} %get-tuple-element.23.grad0) | copy-start | bytes 3145732
  78.5 1.0 copy-start.8
  82.7 1.0 copy-start.9
  83.7 2.7 %collective-permute-start.5 = (bf16[8,4,32,512]{3,2,1,0:T(8,128)(2,1)S(1)}, bf16[8,4,32,512]{3,2,1,0:T(8,128)(2,1)S(1)}, u32[]{:S(2)}, u32[]{:S(2)}) collective-permute-start(bf16[8,4,32,512]{3,2,1,0:T(8,128)(2,1)S(1)} %get-tuple-element.31), channel_id=1, source_target_pairs={{0,16},{16,0},{32,48},{48,32},{64,80},{80,64},{96,112},{112,96},{1... | collective-permute-start | bytes 3145736 | tf_op jit(solution)/shard_map/ppermute | solution.py:47
  83.7 61.0 %collective-permute-start.4 = (bf16[1024,512]{1,0:T(8,128)(2,1)}, bf16[1024,512]{1,0:T(8,128)(2,1)}, u32[]{:S(2)}, u32[]{:S(2)}) collective-permute-start(bf16[1024,512]{1,0:T(8,128)(2,1)} %get-tuple-element.27), channel_id=1, source_target_pairs={{0,1},{1,0},{2,3},{3,2},{4,5},{5,4},{6,7},{7,6},{8,9},{9,8},{10,11... | collective-permute-start | bytes 3145736 | tf_op jit(solution)/shard_map/ppermute | solution.py:47
  87.9 35.3 %all-to-all-start.2 = ((bf16[8,4,32,512]{3,2,1,0:T(8,128)(2,1)}), bf16[8,4,32,512]{3,2,1,0:T(8,128)(2,1)}, u32[]{:S(2)}, u32[]{:S(2)}) async-start(bf16[8,4,32,512]{3,2,1,0:T(8,128)(2,1)} %add_convert_fusion), calls=%async_computation.2 | async-start | bytes 2097152 | tf_op jit(solution)/shard_map/all_to_all | solution.py:222
  95.4 58.1 %collective-permute-start.2 = (bf16[1024,512]{1,0:T(8,128)(2,1)}, bf16[1024,512]{1,0:T(8,128)(2,1)}, u32[]{:S(2)}, u32[]{:S(2)}) collective-permute-start(bf16[1024,512]{1,0:T(8,128)(2,1)} %copy-done.8), channel_id=1, source_target_pairs={{0,8},{1,9},{2,10},{3,11},{4,12},{5,13},{6,14},{7,15},{8,0},{9,1},... | collective-permute-start | bytes 3145736 | tf_op jit(solution)/shard_map/ppermute | solution.py:47
  125.3 34.3 %all-to-all-start.3 = ((bf16[16,32,128]{2,1,0:T(8,128)(2,1)}), bf16[16,32,128]{2,1,0:T(8,128)(2,1)S(1)}, u32[]{:S(2)}, u32[]{:S(2)}) async-start(bf16[16,32,128]{2,1,0:T(8,128)(2,1)} %bitcast.20), calls=%async_computation.3 | async-start | bytes 262144 | tf_op jit(solution)/shard_map/all_to_all | solution.py:225
  144.7 1.2 copy-start.3
  145.9 1.2 copy-start.10
  147.1 1.2 copy-start.13
  148.4 5.1 %copy-start.6 = (f32[1024]{0:T(1024)S(1)}, f32[1024]{0:T(1024)}, u32[]{:S(2)}) copy-start(f32[1024]{0:T(1024)} %param.8) | copy-start | bytes 12292
  153.4 6.1 %copy-start.4 = (f32[4,32,32]{2,1,0:T(8,128)S(1)}, f32[4,32,32]{2,1,0:T(8,128)}, u32[]{:S(2)}) copy-start(f32[4,32,32]{2,1,0:T(8,128)} %constant_dynamic-slice_fusion.operators) | copy-start | bytes 49156
  153.5 6.1 %copy-start.5 = (f32[4,32,32]{2,1,0:T(8,128)S(1)}, f32[4,32,32]{2,1,0:T(8,128)}, u32[]{:S(2)}) copy-start(f32[4,32,32]{2,1,0:T(8,128)} %state.1) | copy-start | bytes 49156
